TPU v7x, 512 devices: a whole 4x4x16 slice. The times are simulated.
512 devices in a mesh: mem: 32 (over z, core), space: 16 (over y, x).
Axes of the slice: x: 4, y: 4, z: 16, core: 2. Of those that a mesh axis runs over, the one named last changes fastest.
Arguments:
- ensemble: bfloat16 [1024, 262144], P('mem', 'space'), may hold values from -420 to 420, as said below
- log_weights: float32 [1024], replicated, may hold values from -405 to -195, as said below
Outputs:
- analysis: bfloat16 [1024, 262144], P('mem', 'space')
Inputs may be any that keep to these rules, and one draw needn't show every extreme that they name: `ensemble`: finite values. `log_weights`: unnormalized log-likelihoods; only differences between members matter.
All inputs are finite; a program needn't handle non-finite values.
Results may differ from a plain program's by a relative error of at most 0.003.
The roundings to bfloat16 on the way count: a program that leaves them out, or rounds other values in their place, can miss the bound.
Values may be sent and summed in bfloat16 or wider, within the bound.
No kernel may reach another device: no remote copies, remote signals or barrier semaphores. Data moves between devices by JAX's collectives and lax.ppermute only.
A program may use at most 64 MiB of HBM per device.

v0:
```python
import jax
import jax.numpy as jnp
from jax import lax
from jax.sharding import PartitionSpec as P

M = 1024
ITERS = 10


def coupling_from(kernel_part, weights_part, total_sum):

    def sweep(step, carry):
        row_scale, col_scale = carry
        row_scale = weights_part / jnp.dot(kernel_part, col_scale, precision=lax.Precision.HIGHEST)
        sums = total_sum(jnp.dot(row_scale, kernel_part, precision=lax.Precision.HIGHEST))
        return (row_scale, 1.0 / M / sums)

    start_col = jnp.ones((kernel_part.shape[1],), jnp.float32)
    row_scale, col_scale = lax.fori_loop(0, ITERS, sweep, (weights_part, start_col))
    return (M * row_scale[:, None] * kernel_part * col_scale[None, :]).astype(jnp.bfloat16)


def per_device(ensemble, log_weights):
    members_dev = ensemble.shape[0]
    cells_total = ensemble.shape[1] * lax.axis_size("space")
    relaid = lax.all_to_all(ensemble, "mem", split_axis=1, concat_axis=0, tiled=True)
    partial_gram = lax.dot_general(
        relaid, relaid, (((1,), (1,)), ((), ())), preferred_element_type=jnp.float32
    )
    weights = jax.nn.softmax(log_weights)
    local_rows = lax.psum_scatter(partial_gram, "mem", scatter_dimension=0, tiled=True)
    gram_rows = lax.psum(local_rows, "space")
    start = lax.axis_index("mem") * members_dev
    own_block = lax.dynamic_slice_in_dim(gram_rows, start, members_dev, 1)
    own_norms = jnp.sum(own_block * jnp.eye(members_dev, dtype=jnp.float32), axis=1)
    all_norms = lax.all_gather(own_norms, "mem", axis=0, tiled=True)
    dist = (own_norms[:, None] + all_norms[None, :] - 2.0 * gram_rows) / cells_total
    dist_total = lax.psum(jnp.sum(dist), "mem")
    mean_dist = dist_total / (M * (M - 1))
    kernel = jnp.exp(-dist / (0.08 * mean_dist))
    weights_rows = lax.dynamic_slice_in_dim(weights, start, members_dev, 0)

    def column_total(values):
        return lax.psum(values, "mem")

    coupling_rows = coupling_from(kernel, weights_rows, column_total)
    coupling = lax.all_gather(coupling_rows, "mem", axis=0, tiled=True)
    mixed = lax.dot_general(
        coupling, relaid, (((0,), (0,)), ((), ())), preferred_element_type=jnp.float32
    )
    mixed = mixed.astype(jnp.bfloat16)
    return lax.all_to_all(mixed, "mem", split_axis=0, concat_axis=1, tiled=True)


def solution(mesh):
    return jax.shard_map(
        per_device,
        mesh=mesh,
        in_specs=(P("mem", "space"), P()),
        out_specs=P("mem", "space"),
        check_vma=False,
    )
```

profile of v0, /device:TPU:1, one launch (start us, length us, event | category | flops | bytes accessed | tf_op | source)
XLA Modules:
  0.0 1010.4 jit_solution(11346003454657286297)
XLA Ops:
  6.5 0.0 reduce-scatter.2.cloned.1.call-start
  6.5 1.4 copy.12
  7.9 72.3 %all_to_all.38 = bf16[32,32,512]{2,0,1:T(8,128)(2,1)S(1)} all-to-all(bf16[32,32,512]{2,0,1:T(8,128)(2,1)S(1)} %bitcast.43), channel_id=1, replica_groups=mesh['mem'=32,'space'=16] {'mem'}, dimensions={1} | all-to-all | bytes 2097152 | tf_op jit(solution)/shard_map/all_to_all | solution.py:26
  80.2 3.2 fusion.6
  83.4 0.0 reduce-scatter.2.cloned.1.call-update
  83.4 0.0 all-reduce.3.cloned.1.call-start
  83.5 1.3 dynamic-slice
  85.3 0.0 copy-done.1
  85.3 0.6 reduce_max.9
  85.9 1.2 fusion.5
  87.2 98.8 %reduce-scatter.2.cloned.1.call-done = f32[32,1024]{1,0:T(8,128)} async-done(((f32[1024,1024]{1,0:T(8,128)}), f32[32,1024]{1,0:T(8,128)}) %reduce-scatter.2.cloned.1.call-update) | async-done | bytes 131088 | tf_op jit(solution)/shard_map/reduce_scatter | solution.py:31
  186.0 0.0 all-reduce.3.cloned.1.call-update
  186.0 0.0 all-gather.2.cloned.1.call-start
  186.1 1.2 fusion.4
  187.3 0.1 dynamic_slice.6
  187.4 114.0 %all-reduce.3.cloned.1.call-done = f32[32,1024]{1,0:T(8,128)} async-done(((f32[32,1024]{1,0:T(8,128)}), f32[32,1024]{1,0:T(8,128)}) %all-reduce.3.cloned.1.call-update) | async-done | bytes 131088 | tf_op jit(solution)/shard_map/psum | solution.py:32
  301.4 1.0 select_reduce_fusion
  302.4 0.2 dynamic-update-slice
  302.7 48.6 %all-reduce = f32[1024]{0:T(1024)S(1)} all-reduce(f32[1024]{0:T(1024)S(1)} %dynamic-update-slice), channel_id=1, replica_groups=mesh['mem'=32,'space'=16] {'mem'}, use_global_device_ids=true, to_apply=%add | all-reduce | flops 1024 | bytes 8192
  351.2 1.7 fusion.3
  352.9 0.5 copy.16
  353.4 47.1 %psum.22 = f32[]{:T(128)} all-reduce(f32[]{:T(128)} %fusion.3), channel_id=1, replica_groups=mesh['mem'=32,'space'=16] {'mem'}, use_global_device_ids=true, to_apply=%region_6.0 | all-reduce | flops 1 | bytes 8 | tf_op jit(solution)/shard_map/psum | solution.py:38
  401.2 1.0 divide_exponential_fusion
  402.2 462.6 %while.13 = (s32[]{:T(128)}, f32[32]{0:T(128)}, f32[1024]{0:T(1024)S(1)}, f32[32,1024]{1,0:T(8,128)S(1)}, f32[32]{0:T(128)S(1)}, /*index=5*/s32[]{:T(128)}, s32[]{:T(128)}) while((s32[]{:T(128)}, f32[32]{0:T(128)}, f32[1024]{0:T(1024)S(1)}, f32[32,1024]{1,0:T(8,128)S(1)}, f32[32]{0:T(128)S(1)}, /*index=5*/s32[]{:T(128)}, ...), condition=%wide.region_9.0_spmd.clone, body=%wide.region_7.0_spmd.clone.sunk | while | flops 789539 | bytes 295923 | solution.py:19
  402.2 0.2 fusion.24
  402.4 0.2 fusion.25
  402.6 45.8 %psum.25 = f32[1024]{0:T(1024)S(1)} all-reduce(f32[1024]{0:T(1024)S(1)} %bitcast.49), channel_id=1, replica_groups=mesh['mem'=32,'space'=16] {'mem'}, use_global_device_ids=true, to_apply=%region_8.0 | all-reduce | flops 1024 | bytes 8192 | tf_op jit(solution)/shard_map/while/body/eval_jaxpr/psum | solution.py:44
  448.4 0.0 copy-done.2
  448.5 0.2 fusion.24
  448.7 0.2 fusion.25
  448.9 45.8 %psum.25 = f32[1024]{0:T(1024)S(1)} all-reduce(f32[1024]{0:T(1024)S(1)} %bitcast.49), channel_id=1, replica_groups=mesh['mem'=32,'space'=16] {'mem'}, use_global_device_ids=true, to_apply=%region_8.0 | all-reduce | flops 1024 | bytes 8192 | tf_op jit(solution)/shard_map/while/body/eval_jaxpr/psum | solution.py:44
  494.7 0.0 copy-done.2
  494.7 0.2 fusion.24
  494.9 0.2 fusion.25
  495.2 45.8 %psum.25 = f32[1024]{0:T(1024)S(1)} all-reduce(f32[1024]{0:T(1024)S(1)} %bitcast.49), channel_id=1, replica_groups=mesh['mem'=32,'space'=16] {'mem'}, use_global_device_ids=true, to_apply=%region_8.0 | all-reduce | flops 1024 | bytes 8192 | tf_op jit(solution)/shard_map/while/body/eval_jaxpr/psum | solution.py:44
  541.0 0.2 fusion.24
  541.2 0.2 fusion.25
  541.4 45.8 %psum.25 = f32[1024]{0:T(1024)S(1)} all-reduce(f32[1024]{0:T(1024)S(1)} %bitcast.49), channel_id=1, replica_groups=mesh['mem'=32,'space'=16] {'mem'}, use_global_device_ids=true, to_apply=%region_8.0 | all-reduce | flops 1024 | bytes 8192 | tf_op jit(solution)/shard_map/while/body/eval_jaxpr/psum | solution.py:44
  587.3 0.2 fusion.24
  587.4 0.2 fusion.25
  587.7 45.8 %psum.25 = f32[1024]{0:T(1024)S(1)} all-reduce(f32[1024]{0:T(1024)S(1)} %bitcast.49), channel_id=1, replica_groups=mesh['mem'=32,'space'=16] {'mem'}, use_global_device_ids=true, to_apply=%region_8.0 | all-reduce | flops 1024 | bytes 8192 | tf_op jit(solution)/shard_map/while/body/eval_jaxpr/psum | solution.py:44
  633.5 0.2 fusion.24
  633.7 0.2 fusion.25
  633.9 45.8 %psum.25 = f32[1024]{0:T(1024)S(1)} all-reduce(f32[1024]{0:T(1024)S(1)} %bitcast.49), channel_id=1, replica_groups=mesh['mem'=32,'space'=16] {'mem'}, use_global_device_ids=true, to_apply=%region_8.0 | all-reduce | flops 1024 | bytes 8192 | tf_op jit(solution)/shard_map/while/body/eval_jaxpr/psum | solution.py:44
  679.8 0.2 fusion.24
  680.0 0.2 fusion.25
  680.2 45.8 %psum.25 = f32[1024]{0:T(1024)S(1)} all-reduce(f32[1024]{0:T(1024)S(1)} %bitcast.49), channel_id=1, replica_groups=mesh['mem'=32,'space'=16] {'mem'}, use_global_device_ids=true, to_apply=%region_8.0 | all-reduce | flops 1024 | bytes 8192 | tf_op jit(solution)/shard_map/while/body/eval_jaxpr/psum | solution.py:44
  726.0 0.2 fusion.24
  726.2 0.2 fusion.25
  726.5 45.8 %psum.25 = f32[1024]{0:T(1024)S(1)} all-reduce(f32[1024]{0:T(1024)S(1)} %bitcast.49), channel_id=1, replica_groups=mesh['mem'=32,'space'=16] {'mem'}, use_global_device_ids=true, to_apply=%region_8.0 | all-reduce | flops 1024 | bytes 8192 | tf_op jit(solution)/shard_map/while/body/eval_jaxpr/psum | solution.py:44
  772.3 0.2 fusion.24
  772.5 0.2 fusion.25
  772.7 45.8 %psum.25 = f32[1024]{0:T(1024)S(1)} all-reduce(f32[1024]{0:T(1024)S(1)} %bitcast.49), channel_id=1, replica_groups=mesh['mem'=32,'space'=16] {'mem'}, use_global_device_ids=true, to_apply=%region_8.0 | all-reduce | flops 1024 | bytes 8192 | tf_op jit(solution)/shard_map/while/body/eval_jaxpr/psum | solution.py:44
  818.6 0.2 fusion.24
  818.7 0.2 fusion.25
  819.0 45.8 %psum.25 = f32[1024]{0:T(1024)S(1)} all-reduce(f32[1024]{0:T(1024)S(1)} %bitcast.49), channel_id=1, replica_groups=mesh['mem'=32,'space'=16] {'mem'}, use_global_device_ids=true, to_apply=%region_8.0 | all-reduce | flops 1024 | bytes 8192 | tf_op jit(solution)/shard_map/while/body/eval_jaxpr/psum | solution.py:44
  864.8 0.6 broadcast_multiply_fusion
  865.4 0.0 copy-done
  865.4 0.7 multiply_convert_fusion
  866.1 0.0 all-gather.2.cloned.1.call-update
  866.2 70.0 %all-gather.2.cloned.1.call-done = bf16[1024,1024]{1,0:T(8,128)(2,1)} async-done(((bf16[32,1024]{1,0:T(8,128)(2,1)}), bf16[1024,1024]{1,0:T(8,128)(2,1)}) %all-gather.2.cloned.1.call-update) | async-done | bytes 2097168 | tf_op jit(solution)/shard_map/all_gather | solution.py:47
  936.2 2.9 convolution_convert_fusion
  939.0 63.8 %all_to_all.39 = bf16[32,32,512]{2,1,0:T(8,128)(2,1)S(1)} all-to-all(bf16[32,32,512]{2,1,0:T(8,128)(2,1)S(1)} %bitcast.47), channel_id=1, replica_groups=mesh['mem'=32,'space'=16] {'mem'}, dimensions={0} | all-to-all | bytes 2097152 | tf_op jit(solution)/shard_map/all_to_all | solution.py:52
  1002.8 1.1 copy.10
  (42 shorter events, 0.2 us)
Async XLA Ops:
  6.5 179.5 %reduce-scatter.2.cloned.1.call-start = ((), (), s32[]{:S(2)}) async-start(), calls=%async_computation.3 | async-start | bytes 4325376 | tf_op jit(solution)/shard_map/reduce_scatter | solution.py:31
  83.4 1.9 copy-start.1
  83.4 218.0 %all-reduce.3.cloned.1.call-start = ((), (), s32[]{:S(2)}) async-start(), calls=%async_computation.4 | async-start | bytes 262144 | tf_op jit(solution)/shard_map/psum | solution.py:32
  186.0 750.1 %all-gather.2.cloned.1.call-start = ((), (), s32[]{:S(2)}) async-start(), calls=%async_computation.5 | async-start | bytes 2162688 | tf_op jit(solution)/shard_map/all_gather | solution.py:47
  301.4 564.0 %copy-start = (f32[32,1024]{1,0:T(8,128)S(1)}, f32[32,1024]{1,0:T(8,128)}, u32[]{:S(2)}) copy-start(f32[32,1024]{1,0:T(8,128)} %all-reduce.3.cloned.1.call-done) | copy-start | bytes 393220
  402.4 46.0 %copy-start.2 = (f32[32]{0:T(128)}, f32[32]{0:T(128)S(1)}, u32[]{:S(2)}) copy-start(f32[32]{0:T(128)S(1)} %fusion.24) | copy-start | bytes 388 | tf_op jit(solution)/shard_map/while
  448.7 46.0 %copy-start.2 = (f32[32]{0:T(128)}, f32[32]{0:T(128)S(1)}, u32[]{:S(2)}) copy-start(f32[32]{0:T(128)S(1)} %fusion.24) | copy-start | bytes 388 | tf_op jit(solution)/shard_map/while
  494.9 46.0 %copy-start.2 = (f32[32]{0:T(128)}, f32[32]{0:T(128)S(1)}, u32[]{:S(2)}) copy-start(f32[32]{0:T(128)S(1)} %fusion.24) | copy-start | bytes 388 | tf_op jit(solution)/shard_map/while
  541.2 46.0 %copy-start.2 = (f32[32]{0:T(128)}, f32[32]{0:T(128)S(1)}, u32[]{:S(2)}) copy-start(f32[32]{0:T(128)S(1)} %fusion.24) | copy-start | bytes 388 | tf_op jit(solution)/shard_map/while
  587.4 46.0 %copy-start.2 = (f32[32]{0:T(128)}, f32[32]{0:T(128)S(1)}, u32[]{:S(2)}) copy-start(f32[32]{0:T(128)S(1)} %fusion.24) | copy-start | bytes 388 | tf_op jit(solution)/shard_map/while
  633.7 46.0 %copy-start.2 = (f32[32]{0:T(128)}, f32[32]{0:T(128)S(1)}, u32[]{:S(2)}) copy-start(f32[32]{0:T(128)S(1)} %fusion.24) | copy-start | bytes 388 | tf_op jit(solution)/shard_map/while
  680.0 46.0 %copy-start.2 = (f32[32]{0:T(128)}, f32[32]{0:T(128)S(1)}, u32[]{:S(2)}) copy-start(f32[32]{0:T(128)S(1)} %fusion.24) | copy-start | bytes 388 | tf_op jit(solution)/shard_map/while
  726.2 46.0 %copy-start.2 = (f32[32]{0:T(128)}, f32[32]{0:T(128)S(1)}, u32[]{:S(2)}) copy-start(f32[32]{0:T(128)S(1)} %fusion.24) | copy-start | bytes 388 | tf_op jit(solution)/shard_map/while
  772.5 46.0 %copy-start.2 = (f32[32]{0:T(128)}, f32[32]{0:T(128)S(1)}, u32[]{:S(2)}) copy-start(f32[32]{0:T(128)S(1)} %fusion.24) | copy-start | bytes 388 | tf_op jit(solution)/shard_map/while
  818.7 46.0 %copy-start.2 = (f32[32]{0:T(128)}, f32[32]{0:T(128)S(1)}, u32[]{:S(2)}) copy-start(f32[32]{0:T(128)S(1)} %fusion.24) | copy-start | bytes 388 | tf_op jit(solution)/shard_map/while
Sparse Core Ops, SparseCore 0:
  83.5 102.4 reduce-scatter.1
  189.2 112.2 all-reduce.2
  866.3 69.8 all-gather.1
where the time goes:
time: 1010 us
  blocking collectives  690 us (68%)
  waiting for transfers between devices  283 us (28%)
  between operations  14.4 us (1%)
  matrix products  10.1 us (1%)
    psum x10, blocking collectives, column_total(): return lax.psum(values, 'mem')  458 us
    psum x1, waiting for transfers between devices, per_device(): gram_rows = lax.psum(local_rows, 'space')  114 us
    reduce_scatter x1, waiting for transfers between devices, per_device(): lax.psum_scatter(partial_gram, 'mem', scatter_dimension=0, tiled=True)  98.8 us
    all_to_all x1, blocking collectives, per_device(): lax.all_to_all(ensemble, 'mem', split_axis=1, concat_axis=0, tiled=True)  72.3 us
    all_gather x1, waiting for transfers between devices, per_device(): coupling = lax.all_gather(coupling_rows, 'mem', axis=0, tiled=True)  70 us
    all_to_all x1, blocking collectives, per_device(): return lax.all_to_all(mixed, 'mem', split_axis=0, concat_axis=1, tiled=True)  63.8 us
    unnamed x1, blocking collectives  48.6 us
    psum x1, blocking collectives, per_device(): dist_total = lax.psum(jnp.sum(dist), 'mem')  47.1 us
  transfers between devices with their start and end apart: 3, of which 3 were waited for; matrix products, arithmetic and copies ran while one was open for 0% of the time, Pallas kernels for 0%

commit v1 on v0

v1 whole, which is shorter than its diff:
```python
import functools

import jax
import jax.numpy as jnp
from jax import lax
from jax.experimental import pallas as pl
from jax.experimental.pallas import tpu as pltpu
from jax.sharding import Mesh
from jax.sharding import PartitionSpec as P

M = 1024
ITERS = 10
T = 128
NB = M // T
TILES = [(i, j) for i in range(NB) for j in range(i, NB)]
HALF = len(TILES) // 2
ROWS = HALF * T
GROUP = 32
MEM = ("z", "core")
PLANE = ("y", "x")


def eye_mask():
    return lax.broadcasted_iota(jnp.int32, (T, T), 0) == lax.broadcasted_iota(jnp.int32, (T, T), 1)


def distance_kernel(core_ref, relaid_ref, keep_ref, send_ref, packed, sems):
    core = core_ref[0]
    eye = eye_mask()
    norm_row = {}
    for i in reversed(range(NB)):
        rows = relaid_ref[i * T:(i + 1) * T, :]
        strip = lax.dot_general(
            rows, relaid_ref[i * T:, :], (((1,), (1,)), ((), ())), preferred_element_type=jnp.float32
        )
        own = jnp.where(eye, strip[:, :T], 0.0)
        norm_row[i] = jnp.sum(own, axis=0, keepdims=True)
        norm_col = jnp.sum(own, axis=1, keepdims=True)
        for j in range(i, NB):
            tile = TILES.index((i, j))
            half, slot = divmod(tile, HALF)
            gram = strip[:, (j - i) * T:(j - i + 1) * T]
            packed[half, slot * T:(slot + 1) * T, :] = norm_col + norm_row[j] - 2.0 * gram
    keep = pltpu.make_async_copy(packed.at[core], keep_ref, sems.at[0])
    send = pltpu.make_async_copy(packed.at[1 - core], send_ref, sems.at[1])
    send.start()
    keep.start()
    send.wait()
    keep.wait()


def partial_distances(core, relaid):
    shape = jax.ShapeDtypeStruct((ROWS, T), jnp.float32)
    return pl.pallas_call(
        distance_kernel,
        out_shape=(shape, shape),
        grid_spec=pltpu.PrefetchScalarGridSpec(
            num_scalar_prefetch=1,
            grid=(1,),
            in_specs=[pl.BlockSpec(relaid.shape, lambda g, c: (0, 0))],
            out_specs=(pl.BlockSpec(memory_space=pl.ANY), pl.BlockSpec(memory_space=pl.ANY)),
            scratch_shapes=[
                pltpu.VMEM((2, ROWS, T), jnp.float32),
                pltpu.SemaphoreType.DMA((2,)),
            ],
        ),
        compiler_params=pltpu.CompilerParams(vmem_limit_bytes=32 << 20),
        name="distances",
    )(core, relaid)


def analysis_kernel(core_ref, own_ref, other_ref, logw_ref, relaid_ref, out_ref,
                    packed, kern, weight, scale, coup, sems):
    core = core_ref[0]
    first = pltpu.make_async_copy(own_ref, packed.at[core], sems.at[0])
    second = pltpu.make_async_copy(other_ref, packed.at[1 - core], sems.at[1])
    first.start()
    second.start()
    eye = eye_mask()

    def to_column(row):
        return jnp.broadcast_to(jnp.sum(jnp.where(eye, row, 0.0), axis=1, keepdims=True), (T, T))

    logw = logw_ref[...]
    expw = jnp.exp(logw - jnp.max(logw, axis=1, keepdims=True))
    weights = expw / jnp.sum(expw, axis=1, keepdims=True)
    for i in range(NB):
        weight[i * T:(i + 1) * T, :] = to_column(weights[:, i * T:(i + 1) * T])

    first.wait()
    second.wait()

    def tile_of(i, j):
        half, slot = divmod(TILES.index((i, j)), HALF)
        return packed[half, slot * T:(slot + 1) * T, :]

    diagonal = jnp.zeros((8, T), jnp.float32)
    upper = jnp.zeros((8, T), jnp.float32)
    for i, j in TILES:
        part = jnp.sum(tile_of(i, j).reshape(T // 8, 8, T), axis=0)
        if i == j:
            diagonal += part
        else:
            upper += part
    total = jnp.sum(jnp.sum(diagonal + 2.0 * upper, axis=0, keepdims=True), axis=1, keepdims=True)
    mean = total / (M * (M - 1))
    rate = -1.0 / (0.08 * mean)
    for i, j in TILES:
        value = jnp.exp(tile_of(i, j) * rate)
        kern[i * T:(i + 1) * T, j * T:(j + 1) * T] = value
        if i != j:
            kern[j * T:(j + 1) * T, i * T:(i + 1) * T] = value.T

    steps = M // (8 * GROUP)

    def sweep(step, cols):
        wide = [jnp.broadcast_to(c, (8, T)) for c in cols]

        def block(b, sums):
            base = pl.multiple_of(b * (8 * GROUP), 8 * GROUP)
            row_scale = []
            for g in range(GROUP):
                rows = pl.ds(base + 8 * g, 8)
                acc = kern[rows, 0:T] * wide[0]
                for l in range(1, NB):
                    acc += kern[rows, l * T:(l + 1) * T] * wide[l]
                r = weight[rows, :] / jnp.sum(acc, axis=1, keepdims=True)
                scale[rows, :] = r
                row_scale.append(r)
            sums = list(sums)
            for g in range(GROUP):
                rows = pl.ds(base + 8 * g, 8)
                for l in range(NB):
                    sums[l] += kern[rows, l * T:(l + 1) * T] * row_scale[g]
            return tuple(sums)

        zeros = tuple(jnp.zeros((8, T), jnp.float32) for _ in range(NB))
        sums = lax.fori_loop(0, steps, block, zeros)
        return tuple((1.0 / M) / jnp.sum(s, axis=0, keepdims=True) for s in sums)

    ones = tuple(jnp.ones((1, T), jnp.float32) for _ in range(NB))
    cols = lax.fori_loop(0, ITERS, sweep, ones)

    row_scale = [
        M * jnp.sum(jnp.where(eye, scale[i * T:(i + 1) * T, :], 0.0), axis=0, keepdims=True)
        for i in range(NB)
    ]
    for j in range(NB):
        col_scale = to_column(cols[j])
        for i in range(NB):
            value = row_scale[i] * kern[j * T:(j + 1) * T, i * T:(i + 1) * T] * col_scale
            coup[j * T:(j + 1) * T, i * T:(i + 1) * T] = value.astype(jnp.bfloat16)
    for j in range(0, NB, 2):
        mixed = jnp.dot(
            coup[j * T:(j + 2) * T, :], relaid_ref[...], preferred_element_type=jnp.float32
        )
        out_ref[j * T:(j + 2) * T, :] = mixed.astype(jnp.bfloat16)


def analysis_members(core, own, other, log_weights, relaid):
    return pl.pallas_call(
        analysis_kernel,
        out_shape=jax.ShapeDtypeStruct(relaid.shape, jnp.bfloat16),
        grid_spec=pltpu.PrefetchScalarGridSpec(
            num_scalar_prefetch=1,
            grid=(1,),
            in_specs=[
                pl.BlockSpec(memory_space=pl.ANY),
                pl.BlockSpec(memory_space=pl.ANY),
                pl.BlockSpec((1, M), lambda g, c: (0, 0)),
                pl.BlockSpec(relaid.shape, lambda g, c: (0, 0)),
            ],
            out_specs=pl.BlockSpec(relaid.shape, lambda g, c: (0, 0)),
            scratch_shapes=[
                pltpu.VMEM((2, ROWS, T), jnp.float32),
                pltpu.VMEM((M, M), jnp.float32),
                pltpu.VMEM((M, T), jnp.float32),
                pltpu.VMEM((M, T), jnp.float32),
                pltpu.VMEM((M, M), jnp.bfloat16),
                pltpu.SemaphoreType.DMA((2,)),
            ],
        ),
        compiler_params=pltpu.CompilerParams(vmem_limit_bytes=40 << 20),
        name="analysis",
    )(core, own, other, log_weights, relaid)


def per_device(ensemble, log_weights):
    core = lax.axis_index("core").reshape(1)
    plane = lax.axis_size("y") * lax.axis_size("x")
    depth = lax.axis_size("z")
    swap = [(0, 1), (1, 0)]
    relaid = lax.all_to_all(ensemble, MEM, split_axis=1, concat_axis=0, tiled=True)
    keep, send = partial_distances(core, relaid)
    half = keep + lax.ppermute(send, "core", swap)
    parts = lax.all_to_all(half.reshape(plane, ROWS // plane, T), PLANE, 0, 0, tiled=True)
    strip = jnp.sum(parts, axis=0)
    pieces = lax.all_to_all(strip.reshape(depth, -1, T), "z", 0, 0, tiled=True)
    piece = jnp.sum(pieces, axis=0)
    spread = jnp.broadcast_to(piece[None], (depth,) + piece.shape)
    strip = lax.all_to_all(spread, "z", 0, 0, tiled=True).reshape(ROWS // plane, T)
    spread = jnp.broadcast_to(strip[None], (plane,) + strip.shape)
    own = lax.all_to_all(spread, PLANE, 0, 0, tiled=True).reshape(ROWS, T)
    other = lax.ppermute(own, "core", swap)
    mixed = analysis_members(core, own, other, log_weights.reshape(1, M), relaid)
    return lax.all_to_all(mixed, MEM, split_axis=0, concat_axis=1, tiled=True)


def solution(mesh):
    fine = Mesh(mesh.devices.reshape(16, 2, 4, 4), ("z", "core", "y", "x"))
    return jax.shard_map(
        per_device,
        mesh=fine,
        in_specs=(P(MEM, PLANE), P()),
        out_specs=P(MEM, PLANE),
        check_vma=False,
    )
```

time: 1010 us -> 240 us (0.24)
  blocking collectives: 690 us -> 136 us
  waiting for transfers between devices: 283 us -> 60.6 us
  starting transfers between devices: 0.08 us -> 26 us
  between operations: 14.4 us -> 0.08 us
  Pallas kernels: 0 us -> 12.3 us
  matrix products: 10.1 us -> 0 us
    psum x11 -> x0, blocking collectives: 505 us -> none  [the longest x10 458 us: column_total(): return lax.psum(values, 'mem')]
    psum x1 -> x0, waiting for transfers between devices: 114 us -> none  [per_device(): gram_rows = lax.psum(local_rows, 'space')]
    reduce_scatter x1 -> x0, waiting for transfers between devices: 98.8 us -> none  [per_device(): lax.psum_scatter(partial_gram, 'mem', scatter_dimension=0, tiled=True)]
    all_gather x1 -> x0, waiting for transfers between devices: 70 us -> none  [per_device(): coupling = lax.all_gather(coupling_rows, 'mem', axis=0, tiled=True)]
    all_to_all x0 -> x1, waiting for transfers between devices: none -> 55.7 us  [per_device(): lax.all_to_all(ensemble, MEM, split_axis=1, concat_axis=0, tiled=True)]
    unnamed x1 -> x0, blocking collectives: 48.6 us -> none
    all_to_all x0 -> x1, starting transfers between devices: none -> 16.7 us  [per_device(): lax.all_to_all(ensemble, MEM, split_axis=1, concat_axis=0, tiled=True)]
    pallas_call x0 -> x2, Pallas kernels: none -> 12.3 us  [the longest x1 10.2 us: analysis_members(): pl.pallas_call(analysis_kernel, out_shape=jax.ShapeDtypeStruct(relaid.sha...]
where the time goes in v1:
time: 240 us; the launch traced here: 239 us
  blocking collectives  136 us (57%)
  waiting for transfers between devices  60.6 us (25%)
  starting transfers between devices  26 us (11%)
  Pallas kernels  12.3 us (5%)
  local copies, waits for them, and re-layouts  3.52 us (1%)
    all_to_all x1, blocking collectives, per_device(): return lax.all_to_all(mixed, MEM, split_axis=0, concat_axis=1, tiled=True)  61.8 us
    all_to_all x1, waiting for transfers between devices, per_device(): lax.all_to_all(ensemble, MEM, split_axis=1, concat_axis=0, tiled=True)  55.7 us
    all_to_all x1, blocking collectives, per_device(): lax.all_to_all(half.reshape(plane, ROWS // plane, T), PLANE, 0, 0, tiled=...  24.6 us
    all_to_all x1, blocking collectives, per_device(): own = lax.all_to_all(spread, PLANE, 0, 0, tiled=True).reshape(ROWS, T)  18.3 us
    all_to_all x1, blocking collectives, per_device(): lax.all_to_all(spread, 'z', 0, 0, tiled=True).reshape(ROWS // plane, T)  17.2 us
    all_to_all x1, starting transfers between devices, per_device(): lax.all_to_all(ensemble, MEM, split_axis=1, concat_axis=0, tiled=True)  16.7 us
    all_to_all x1, blocking collectives, per_device(): pieces = lax.all_to_all(strip.reshape(depth, -1, T), 'z', 0, 0, tiled=True)  14.6 us
    pallas_call x1, Pallas kernels, analysis_members(): pl.pallas_call(analysis_kernel, out_shape=jax.ShapeDtypeStruct(relaid.sha...  10.2 us
  transfers between devices with their start and end apart: 3, of which 3 were waited for; matrix products, arithmetic and copies ran while one was open for 0% of the time, Pallas kernels for 0%

profile of v1, /device:TPU:1, one launch (start us, length us, event | category | flops | bytes accessed | tf_op | source)
XLA Modules:
  0.0 239.3 jit_solution(17410611418874379912)
XLA Ops:
  0.0 2.3 copy.10
  2.3 16.7 %all-to-all-start = ((bf16[32,32,512]{2,0,1:T(8,128)(2,1)}), bf16[32,32,512]{2,0,1:T(8,128)(2,1)S(1)}, u32[]{:S(2)}, u32[]{:S(2)}) async-start(bf16[32,32,512]{2,0,1:T(8,128)(2,1)} %bitcast.14), calls=%async_computation | async-start | bytes 2097152 | tf_op jit(solution)/shard_map/all_to_all | solution.py:193
  19.1 55.7 %all-to-all-done = bf16[32,32,512]{2,0,1:T(8,128)(2,1)S(1)} async-done(((bf16[32,32,512]{2,0,1:T(8,128)(2,1)}), bf16[32,32,512]{2,0,1:T(8,128)(2,1)S(1)}, u32[]{:S(2)}, u32[]{:S(2)}) %all-to-all-start) | async-done | bytes 1048608 | tf_op jit(solution)/shard_map/all_to_all | solution.py:193
  74.8 2.1 distances.1
  76.9 2.4 %collective-permute-start = (f32[2304,128]{1,0:T(8,128)S(1)}, f32[2304,128]{1,0:T(8,128)S(1)}, u32[]{:S(2)}, u32[]{:S(2)}) collective-permute-start(f32[2304,128]{1,0:T(8,128)S(1)} %get-tuple-element.8), channel_id=1, source_target_pairs={{0,16},{16,0},{1,17},{17,1},{2,18},{18,2},{3,19},{19,3},{4,20},{20... | collective-permute-start | bytes 3538952 | tf_op jit(solution)/shard_map/ppermute | solution.py:195
  79.3 2.5 %collective-permute-done = f32[2304,128]{1,0:T(8,128)S(1)} collective-permute-done((f32[2304,128]{1,0:T(8,128)S(1)}, f32[2304,128]{1,0:T(8,128)S(1)}, u32[]{:S(2)}, u32[]{:S(2)}) %collective-permute-start) | collective-permute-done | bytes 1179680 | tf_op jit(solution)/shard_map/ppermute | solution.py:195
  81.8 0.2 add.3
  81.9 24.6 %all_to_all.58 = f32[16,144,128]{2,1,0:T(8,128)S(1)} all-to-all(f32[16,144,128]{2,1,0:T(8,128)S(1)} %bitcast.21), channel_id=1, replica_groups=mesh['z'=16,'core'=2,'y'=4,'x'=4] {'y','x'}, dimensions={0} | all-to-all | bytes 2359296 | tf_op jit(solution)/shard_map/all_to_all | solution.py:196
  106.5 0.1 reduce_sum.18
  106.6 14.6 %all_to_all.59 = f32[16,9,128]{2,1,0:T(8,128)S(1)} all-to-all(f32[16,9,128]{2,1,0:T(8,128)S(1)} %reshape.25), channel_id=1, replica_groups=mesh['z'=16,'core'=2,'y'=4,'x'=4] {'z'}, dimensions={0} | all-to-all | bytes 147456 | tf_op jit(solution)/shard_map/all_to_all | solution.py:198
  121.2 17.2 %all_to_all.60 = f32[16,9,128]{2,1,0:T(8,128)S(1)} all-to-all(f32[16,9,128]{2,1,0:T(8,128)S(1)} %broadcast_in_dim.6), channel_id=1, replica_groups=mesh['z'=16,'core'=2,'y'=4,'x'=4] {'z'}, dimensions={0} | all-to-all | bytes 147456 | tf_op jit(solution)/shard_map/all_to_all | solution.py:201
  138.4 0.1 broadcast_in_dim.15
  138.5 0.0 copy-start
  138.5 18.3 %all_to_all.61 = f32[16,144,128]{2,1,0:T(8,128)S(1)} all-to-all(f32[16,144,128]{2,1,0:T(8,128)S(1)} %broadcast_in_dim.15), channel_id=1, replica_groups=mesh['z'=16,'core'=2,'y'=4,'x'=4] {'y','x'}, dimensions={0} | all-to-all | bytes 2359296 | tf_op jit(solution)/shard_map/all_to_all | solution.py:203
  156.8 6.9 %collective-permute-start.1 = (f32[2304,128]{1,0:T(8,128)S(1)}, f32[2304,128]{1,0:T(8,128)S(1)}, u32[]{:S(2)}, u32[]{:S(2)}) collective-permute-start(f32[2304,128]{1,0:T(8,128)S(1)} %bitcast.17), channel_id=1, source_target_pairs={{0,16},{16,0},{1,17},{17,1},{2,18},{18,2},{3,19},{19,3},{4,20},{20... | collective-permute-start | bytes 3538952 | tf_op jit(solution)/shard_map/ppermute | solution.py:204
  163.7 2.5 %collective-permute-done.1.other_ref = f32[2304,128]{1,0:T(8,128)S(1)} collective-permute-done((f32[2304,128]{1,0:T(8,128)S(1)}, f32[2304,128]{1,0:T(8,128)S(1)}, u32[]{:S(2)}, u32[]{:S(2)}) %collective-permute-start.1) | collective-permute-done | bytes 1179680 | tf_op jit(solution)/shard_map/ppermute | solution.py:204
  166.1 0.0 copy-done
  166.1 10.2 %analysis.1 = bf16[1024,512]{1,0:T(8,128)(2,1)S(1)} custom-call(s32[1]{0:T(128)} %bitcast.core_ref, f32[2304,128]{1,0:T(8,128)S(1)} %bitcast.18, f32[2304,128]{1,0:T(8,128)S(1)} %collective-permute-done.1.other_ref, f32[1,1024]{1,0:T(1,128)S(1)} %bitcast.20, bf16[1024,512]{1,0:T(8,128)(2,1)S(1)} %bitcast.16), custom_call_target="tpu_custom_call" | custom-call | tf_op jit(solution)/shard_map/analysis/pallas_call | solution.py:161
  176.4 61.8 %all_to_all.62 = bf16[32,32,512]{2,1,0:T(8,128)(2,1)S(1)} all-to-all(bf16[32,32,512]{2,1,0:T(8,128)(2,1)S(1)} %bitcast.19), channel_id=1, replica_groups=mesh['z'=16,'core'=2,'y'=4,'x'=4] {'z','core'}, dimensions={0} | all-to-all | bytes 2097152 | tf_op jit(solution)/shard_map/all_to_all | solution.py:206
  238.2 1.1 copy.8
  (4 shorter events, 0.1 us)
Async XLA Ops:
  2.3 72.5 %all-to-all-start = ((bf16[32,32,512]{2,0,1:T(8,128)(2,1)}), bf16[32,32,512]{2,0,1:T(8,128)(2,1)S(1)}, u32[]{:S(2)}, u32[]{:S(2)}) async-start(bf16[32,32,512]{2,0,1:T(8,128)(2,1)} %bitcast.14), calls=%async_computation | async-start | bytes 2097152 | tf_op jit(solution)/shard_map/all_to_all | solution.py:193
  76.9 4.9 %collective-permute-start = (f32[2304,128]{1,0:T(8,128)S(1)}, f32[2304,128]{1,0:T(8,128)S(1)}, u32[]{:S(2)}, u32[]{:S(2)}) collective-permute-start(f32[2304,128]{1,0:T(8,128)S(1)} %get-tuple-element.8), channel_id=1, source_target_pairs={{0,16},{16,0},{1,17},{17,1},{2,18},{18,2},{3,19},{19,3},{4,20},{20... | collective-permute-start | bytes 3538952 | tf_op jit(solution)/shard_map/ppermute | solution.py:195
  138.5 27.7 %copy-start = (f32[1024]{0:T(1024)S(1)}, f32[1024]{0:T(1024)}, u32[]{:S(2)}) copy-start(f32[1024]{0:T(1024)} %param.3) | copy-start | bytes 12292
  156.8 9.3 %collective-permute-start.1 = (f32[2304,128]{1,0:T(8,128)S(1)}, f32[2304,128]{1,0:T(8,128)S(1)}, u32[]{:S(2)}, u32[]{:S(2)}) collective-permute-start(f32[2304,128]{1,0:T(8,128)S(1)} %bitcast.17), channel_id=1, source_target_pairs={{0,16},{16,0},{1,17},{17,1},{2,18},{18,2},{3,19},{19,3},{4,20},{20... | collective-permute-start | bytes 3538952 | tf_op jit(solution)/shard_map/ppermute | solution.py:204

commit v2 on v1

--- a/solution.py
+++ b/solution.py
@@ -1,5 +1,3 @@
-import functools
-
 import jax
 import jax.numpy as jnp
 from jax import lax
@@ -15,6 +13,12 @@
 TILES = [(i, j) for i in range(NB) for j in range(i, NB)]
 HALF = len(TILES) // 2
 ROWS = HALF * T
+HEAD = 8
+PLANE_SIZE = 16
+DEPTH = 16
+STRIP = ROWS // PLANE_SIZE
+PIECE = STRIP // DEPTH
+PAD = 16
 GROUP = 32
 MEM = ("z", "core")
 PLANE = ("y", "x")
@@ -28,6 +32,9 @@
     core = core_ref[0]
     eye = eye_mask()
     norm_row = {}
+    diagonal = jnp.zeros((8, T), jnp.float32)
+    upper = jnp.zeros((8, T), jnp.float32)
+    largest = jnp.zeros((8, T), jnp.float32)
     for i in reversed(range(NB)):
         rows = relaid_ref[i * T:(i + 1) * T, :]
         strip = lax.dot_general(
@@ -40,7 +47,20 @@
             tile = TILES.index((i, j))
             half, slot = divmod(tile, HALF)
             gram = strip[:, (j - i) * T:(j - i + 1) * T]
-            packed[half, slot * T:(slot + 1) * T, :] = norm_col + norm_row[j] - 2.0 * gram
+            value = norm_col + norm_row[j] - 2.0 * gram
+            packed[half, slot * T:(slot + 1) * T, :] = value
+            folded = value.reshape(T // 8, 8, T)
+            largest = jnp.maximum(largest, jnp.max(folded, axis=0))
+            if i == j:
+                diagonal += jnp.sum(folded, axis=0)
+            else:
+                upper += jnp.sum(folded, axis=0)
+    total = jnp.sum(diagonal + 2.0 * upper, keepdims=True)
+    largest = jnp.max(largest, keepdims=True)
+    row = lax.broadcasted_iota(jnp.int32, (HEAD, T), 0)
+    head = jnp.where(row == 0, total, jnp.where(row == 1, largest, 0.0))
+    packed[0, ROWS:, :] = head
+    packed[1, ROWS:, :] = head
     keep = pltpu.make_async_copy(packed.at[core], keep_ref, sems.at[0])
     send = pltpu.make_async_copy(packed.at[1 - core], send_ref, sems.at[1])
     send.start()
@@ -50,7 +70,7 @@
 
 
 def partial_distances(core, relaid):
-    shape = jax.ShapeDtypeStruct((ROWS, T), jnp.float32)
+    shape = jax.ShapeDtypeStruct((ROWS + HEAD, T), jnp.float32)
     return pl.pallas_call(
         distance_kernel,
         out_shape=(shape, shape),
@@ -60,13 +80,75 @@
             in_specs=[pl.BlockSpec(relaid.shape, lambda g, c: (0, 0))],
             out_specs=(pl.BlockSpec(memory_space=pl.ANY), pl.BlockSpec(memory_space=pl.ANY)),
             scratch_shapes=[
-                pltpu.VMEM((2, ROWS, T), jnp.float32),
+                pltpu.VMEM((2, ROWS + HEAD, T), jnp.float32),
                 pltpu.SemaphoreType.DMA((2,)),
             ],
         ),
         compiler_params=pltpu.CompilerParams(vmem_limit_bytes=32 << 20),
         name="distances",
     )(core, relaid)
+
+
+def pack_kernel(keep_ref, recv_ref, out_ref):
+    head = keep_ref[ROWS:, :] + recv_ref[ROWS:, :]
+    bound = jnp.maximum(head[1:2, :], 1e-30)
+    power = jnp.floor(15.0 - jnp.log2(bound))
+    scale = jnp.exp2(power)
+    share = head[0:1, :] * scale * 2.0**-20
+    high = share.astype(jnp.bfloat16).astype(jnp.float32)
+    middle = (share - high).astype(jnp.bfloat16).astype(jnp.float32)
+    low = share - high - middle
+    row = lax.broadcasted_iota(jnp.int32, (PAD, T), 0)
+    tail = jnp.zeros((PAD, T), jnp.float32)
+    for index, value in enumerate((power, high, middle, low)):
+        tail = jnp.where(row == index, value, tail)
+    for p in range(PLANE_SIZE):
+        rows = slice(p * STRIP, (p + 1) * STRIP)
+        out_ref[p, :STRIP, :] = (keep_ref[rows, :] + recv_ref[rows, :]) * scale
+        out_ref[p, STRIP:, :] = tail
+
+
+def strip_kernel(parts_ref, out_ref, strip):
+    acc = jnp.zeros((STRIP, T), jnp.float32)
+    total = jnp.zeros((1, T), jnp.float32)
+    for p in range(PLANE_SIZE):
+        tail = parts_ref[p, STRIP:, :]
+        inverse = jnp.exp2(-tail[0:1, :])
+        acc += parts_ref[p, :STRIP, :] * inverse
+        total += (tail[1:2, :] + tail[2:3, :] + tail[3:4, :]) * inverse
+    strip[:STRIP, :] = acc
+    strip[STRIP:, :] = jnp.zeros((PAD, T), jnp.float32)
+    row = lax.broadcasted_iota(jnp.int32, (PAD, T), 0)
+    total = total * 2.0**20
+    for g in range(DEPTH):
+        piece = strip[g * PIECE:g * PIECE + PAD, :]
+        out_ref[g, :, :] = jnp.where(row == PIECE, total, piece)
+
+
+def entries_kernel(pieces_ref, out_ref):
+    whole = jnp.sum(pieces_ref[...], axis=0)
+    mean = whole[PIECE:PIECE + 1, :] / (M * (M - 1))
+    entries = jnp.exp(whole * (-1.0 / (0.08 * mean))).astype(jnp.bfloat16)
+    for g in range(DEPTH):
+        out_ref[g, :, :] = entries
+
+
+def spread_kernel(pieces_ref, out_ref, strip):
+    for g in range(DEPTH):
+        strip[g * PIECE:g * PIECE + PAD, :] = pieces_ref[g, :, :].astype(jnp.float32)
+    entries = strip[:STRIP, :].astype(jnp.bfloat16)
+    for p in range(PLANE_SIZE):
+        out_ref[p, :, :] = entries
+
+
+def small_call(body, shape, dtype, name, scratch=()):
+    return pl.pallas_call(
+        body,
+        out_shape=jax.ShapeDtypeStruct(shape, dtype),
+        scratch_shapes=scratch,
+        compiler_params=pltpu.CompilerParams(vmem_limit_bytes=16 << 20),
+        name=name,
+    )
 
 
 def analysis_kernel(core_ref, own_ref, other_ref, logw_ref, relaid_ref, out_ref,
@@ -94,19 +176,8 @@
         half, slot = divmod(TILES.index((i, j)), HALF)
         return packed[half, slot * T:(slot + 1) * T, :]
 
-    diagonal = jnp.zeros((8, T), jnp.float32)
-    upper = jnp.zeros((8, T), jnp.float32)
     for i, j in TILES:
-        part = jnp.sum(tile_of(i, j).reshape(T // 8, 8, T), axis=0)
-        if i == j:
-            diagonal += part
-        else:
-            upper += part
-    total = jnp.sum(jnp.sum(diagonal + 2.0 * upper, axis=0, keepdims=True), axis=1, keepdims=True)
-    mean = total / (M * (M - 1))
-    rate = -1.0 / (0.08 * mean)
-    for i, j in TILES:
-        value = jnp.exp(tile_of(i, j) * rate)
+        value = tile_of(i, j).astype(jnp.float32)
         kern[i * T:(i + 1) * T, j * T:(j + 1) * T] = value
         if i != j:
             kern[j * T:(j + 1) * T, i * T:(i + 1) * T] = value.T
@@ -172,7 +243,7 @@
             ],
             out_specs=pl.BlockSpec(relaid.shape, lambda g, c: (0, 0)),
             scratch_shapes=[
-                pltpu.VMEM((2, ROWS, T), jnp.float32),
+                pltpu.VMEM((2, ROWS, T), jnp.bfloat16),
                 pltpu.VMEM((M, M), jnp.float32),
                 pltpu.VMEM((M, T), jnp.float32),
                 pltpu.VMEM((M, T), jnp.float32),
@@ -187,20 +258,19 @@
 
 def per_device(ensemble, log_weights):
     core = lax.axis_index("core").reshape(1)
-    plane = lax.axis_size("y") * lax.axis_size("x")
-    depth = lax.axis_size("z")
     swap = [(0, 1), (1, 0)]
     relaid = lax.all_to_all(ensemble, MEM, split_axis=1, concat_axis=0, tiled=True)
     keep, send = partial_distances(core, relaid)
-    half = keep + lax.ppermute(send, "core", swap)
-    parts = lax.all_to_all(half.reshape(plane, ROWS // plane, T), PLANE, 0, 0, tiled=True)
-    strip = jnp.sum(parts, axis=0)
-    pieces = lax.all_to_all(strip.reshape(depth, -1, T), "z", 0, 0, tiled=True)
-    piece = jnp.sum(pieces, axis=0)
-    spread = jnp.broadcast_to(piece[None], (depth,) + piece.shape)
-    strip = lax.all_to_all(spread, "z", 0, 0, tiled=True).reshape(ROWS // plane, T)
-    spread = jnp.broadcast_to(strip[None], (plane,) + strip.shape)
-    own = lax.all_to_all(spread, PLANE, 0, 0, tiled=True).reshape(ROWS, T)
+    recv = lax.ppermute(send, "core", swap)
+    padded = pltpu.VMEM((STRIP + PAD, T), jnp.float32)
+    halves = small_call(pack_kernel, (PLANE_SIZE, STRIP + PAD, T), jnp.float32, "pack")(keep, recv)
+    parts = lax.all_to_all(halves.astype(jnp.float16), PLANE, 0, 0, tiled=True).astype(jnp.float32)
+    strips = small_call(strip_kernel, (DEPTH, PAD, T), jnp.float32, "strip", [padded])(parts)
+    pieces = lax.all_to_all(strips, "z", 0, 0, tiled=True)
+    entries = small_call(entries_kernel, (DEPTH, PAD, T), jnp.bfloat16, "entries")(pieces)
+    pieces = lax.all_to_all(entries, "z", 0, 0, tiled=True)
+    strips = small_call(spread_kernel, (PLANE_SIZE, STRIP, T), jnp.bfloat16, "spread", [padded])(pieces)
+    own = lax.all_to_all(strips, PLANE, 0, 0, tiled=True).reshape(ROWS, T)
     other = lax.ppermute(own, "core", swap)
     mixed = analysis_members(core, own, other, log_weights.reshape(1, M), relaid)
     return lax.all_to_all(mixed, MEM, split_axis=0, concat_axis=1, tiled=True)

time: 240 us -> 224 us (0.933)
  blocking collectives: 136 us -> 122 us
    all_to_all x4, blocking collectives: 74.6 us -> 63.5 us  [the longest x1 19 us: per_device(): lax.all_to_all(halves.astype(jnp.float16), PLANE, 0, 0, tiled=True)]
    all_to_all x1, blocking collectives: 61.8 us -> 58.8 us  [per_device(): return lax.all_to_all(mixed, MEM, split_axis=0, concat_axis=1, tiled=True)]
where the time goes in v2:
time: 224 us; the launch traced here: 223 us
  blocking collectives  122 us (54%)
  waiting for transfers between devices  59.8 us (27%)
  starting transfers between devices  25.2 us (11%)
  Pallas kernels  12.3 us (5%)
  local copies, waits for them, and re-layouts  3.41 us (2%)
    all_to_all x1, blocking collectives, per_device(): return lax.all_to_all(mixed, MEM, split_axis=0, concat_axis=1, tiled=True)  58.8 us
    all_to_all x1, waiting for transfers between devices, per_device(): lax.all_to_all(ensemble, MEM, split_axis=1, concat_axis=0, tiled=True)  55.7 us
    all_to_all x1, blocking collectives, per_device(): lax.all_to_all(halves.astype(jnp.float16), PLANE, 0, 0, tiled=True)  19 us
    all_to_all x1, blocking collectives, per_device(): pieces = lax.all_to_all(entries, 'z', 0, 0, tiled=True)  16.8 us
    all_to_all x1, starting transfers between devices, per_device(): lax.all_to_all(ensemble, MEM, split_axis=1, concat_axis=0, tiled=True)  16.7 us
    all_to_all x1, blocking collectives, per_device(): pieces = lax.all_to_all(strips, 'z', 0, 0, tiled=True)  14.6 us
    all_to_all x1, blocking collectives, per_device(): own = lax.all_to_all(strips, PLANE, 0, 0, tiled=True).reshape(ROWS, T)  13.2 us
    pallas_call x1, Pallas kernels, analysis_members(): pl.pallas_call(analysis_kernel, out_shape=jax.ShapeDtypeStruct(relaid.sha...  9.6 us
  transfers between devices with their start and end apart: 3, of which 3 were waited for; matrix products, arithmetic and copies ran while one was open for 0% of the time, Pallas kernels for 0%

profile of v2, /device:TPU:1, one launch (start us, length us, event | category | flops | bytes accessed | tf_op | source)
XLA Modules:
  0.0 223.3 jit_solution(7792356770967584137)
XLA Ops:
  0.0 2.3 %copy.8 = bf16[4,32,8,512]{3,2,0,1:T(8,128)(2,1)} copy(bf16[4,32,8,512]{3,2,1,0:T(8,128)(2,1)} %bitcast.21) | data formatting | bytes 2097152 | tf_op jit(solution)/shard_map/all_to_all | solution.py:262
  2.3 16.7 %all-to-all-start = ((bf16[32,32,512]{2,0,1:T(8,128)(2,1)}), bf16[32,32,512]{2,0,1:T(8,128)(2,1)S(1)}, u32[]{:S(2)}, u32[]{:S(2)}) async-start(bf16[32,32,512]{2,0,1:T(8,128)(2,1)} %bitcast.13), calls=%async_computation | async-start | bytes 2097152 | tf_op jit(solution)/shard_map/all_to_all | solution.py:262
  19.1 55.7 %all-to-all-done = bf16[32,32,512]{2,0,1:T(8,128)(2,1)S(1)} async-done(((bf16[32,32,512]{2,0,1:T(8,128)(2,1)}), bf16[32,32,512]{2,0,1:T(8,128)(2,1)S(1)}, u32[]{:S(2)}, u32[]{:S(2)}) %all-to-all-start) | async-done | bytes 1048608 | tf_op jit(solution)/shard_map/all_to_all | solution.py:262
  74.8 2.3 %distances.1 = (f32[2312,128]{1,0:T(8,128)S(1)}, f32[2312,128]{1,0:T(8,128)S(1)}) custom-call(s32[1]{0:T(128)} %bitcast.core_ref, bf16[1024,512]{1,0:T(8,128)(2,1)S(1)} %bitcast.14), custom_call_target="tpu_custom_call" | custom-call | tf_op jit(solution)/shard_map/distances/pallas_call | solution.py:74
  77.2 2.4 %collective-permute-start = (f32[2312,128]{1,0:T(8,128)S(1)}, f32[2312,128]{1,0:T(8,128)S(1)}, u32[]{:S(2)}, u32[]{:S(2)}) collective-permute-start(f32[2312,128]{1,0:T(8,128)S(1)} %get-tuple-element.8), channel_id=1, source_target_pairs={{0,16},{16,0},{1,17},{17,1},{2,18},{18,2},{3,19},{19,3},{4,20},{20... | collective-permute-start | bytes 3551240 | tf_op jit(solution)/shard_map/ppermute | solution.py:264
  79.6 2.5 %collective-permute-done.recv_ref = f32[2312,128]{1,0:T(8,128)S(1)} collective-permute-done((f32[2312,128]{1,0:T(8,128)S(1)}, f32[2312,128]{1,0:T(8,128)S(1)}, u32[]{:S(2)}, u32[]{:S(2)}) %collective-permute-start) | collective-permute-done | bytes 1183776 | tf_op jit(solution)/shard_map/ppermute | solution.py:264
  82.0 0.1 pack.1
  82.2 0.1 convert_element_type.6
  82.3 19.0 %all_to_all.58 = f16[16,160,128]{2,1,0:T(8,128)(2,1)S(1)} all-to-all(f16[16,160,128]{2,1,0:T(8,128)(2,1)S(1)} %convert_element_type.6), channel_id=1, replica_groups=mesh['z'=16,'core'=2,'y'=4,'x'=4] {'y','x'}, dimensions={0} | all-to-all | bytes 1310720 | tf_op jit(solution)/shard_map/all_to_all | solution.py:267
  101.2 0.1 convert_element_type.7.parts_ref
  101.4 0.1 strip.1
  101.5 0.0 copy-start
  101.5 14.6 %all_to_all.59.pieces_ref = f32[16,16,128]{2,1,0:T(8,128)S(1)} all-to-all(f32[16,16,128]{2,1,0:T(8,128)S(1)} %strip.1), channel_id=1, replica_groups=mesh['z'=16,'core'=2,'y'=4,'x'=4] {'z'}, dimensions={0} | all-to-all | bytes 262144 | tf_op jit(solution)/shard_map/all_to_all | solution.py:269
  116.1 16.8 %all_to_all.60.pieces_ref = bf16[16,16,128]{2,1,0:T(8,128)(2,1)S(1)} all-to-all(bf16[16,16,128]{2,1,0:T(8,128)(2,1)S(1)} %entries.1), channel_id=1, replica_groups=mesh['z'=16,'core'=2,'y'=4,'x'=4] {'z'}, dimensions={0} | all-to-all | bytes 131072 | tf_op jit(solution)/shard_map/all_to_all | solution.py:271
  132.9 0.1 spread.1
  132.9 13.2 %all_to_all.61 = bf16[16,144,128]{2,1,0:T(8,128)(2,1)S(1)} all-to-all(bf16[16,144,128]{2,1,0:T(8,128)(2,1)S(1)} %spread.1), channel_id=1, replica_groups=mesh['z'=16,'core'=2,'y'=4,'x'=4] {'y','x'}, dimensions={0} | all-to-all | bytes 1179648 | tf_op jit(solution)/shard_map/all_to_all | solution.py:273
  146.2 6.0 %collective-permute-start.1 = (bf16[2304,128]{1,0:T(8,128)(2,1)S(1)}, bf16[2304,128]{1,0:T(8,128)(2,1)S(1)}, u32[]{:S(2)}, u32[]{:S(2)}) collective-permute-start(bf16[2304,128]{1,0:T(8,128)(2,1)S(1)} %bitcast.17), channel_id=1, source_target_pairs={{0,16},{16,0},{1,17},{17,1},{2,18},{18,2},{3,19},{19,3},{4,20},{20... | collective-permute-start | bytes 1769480 | tf_op jit(solution)/shard_map/ppermute | solution.py:274
  152.2 1.6 collective-permute-done.1.other_ref
  153.8 0.0 copy-done
  153.8 9.6 %analysis.1 = bf16[1024,512]{1,0:T(8,128)(2,1)S(1)} custom-call(s32[1]{0:T(128)} %bitcast.core_ref, bf16[2304,128]{1,0:T(8,128)(2,1)S(1)} %bitcast.18, bf16[2304,128]{1,0:T(8,128)(2,1)S(1)} %collective-permute-done.1.other_ref, f32[1,1024]{1,0:T(1,128)S(1)} %bitcast.19, bf16[1024,512]{1,0:T(8,128)(2,1)S(1)} %bitcast.15), custom_call_target="tpu_custom_call" | custom-call | tf_op jit(solution)/shard_map/analysis/pallas_call | solution.py:232
  163.4 58.8 %all_to_all.62 = bf16[32,32,512]{2,1,0:T(8,128)(2,1)S(1)} all-to-all(bf16[32,32,512]{2,1,0:T(8,128)(2,1)S(1)} %bitcast.16), channel_id=1, replica_groups=mesh['z'=16,'core'=2,'y'=4,'x'=4] {'z','core'}, dimensions={0} | all-to-all | bytes 2097152 | tf_op jit(solution)/shard_map/all_to_all | solution.py:276
  222.2 1.1 copy.6
  (1 shorter events, 0.0 us)
Async XLA Ops:
  2.3 72.5 %all-to-all-start = ((bf16[32,32,512]{2,0,1:T(8,128)(2,1)}), bf16[32,32,512]{2,0,1:T(8,128)(2,1)S(1)}, u32[]{:S(2)}, u32[]{:S(2)}) async-start(bf16[32,32,512]{2,0,1:T(8,128)(2,1)} %bitcast.13), calls=%async_computation | async-start | bytes 2097152 | tf_op jit(solution)/shard_map/all_to_all | solution.py:262
  77.2 4.9 %collective-permute-start = (f32[2312,128]{1,0:T(8,128)S(1)}, f32[2312,128]{1,0:T(8,128)S(1)}, u32[]{:S(2)}, u32[]{:S(2)}) collective-permute-start(f32[2312,128]{1,0:T(8,128)S(1)} %get-tuple-element.8), channel_id=1, source_target_pairs={{0,16},{16,0},{1,17},{17,1},{2,18},{18,2},{3,19},{19,3},{4,20},{20... | collective-permute-start | bytes 3551240 | tf_op jit(solution)/shard_map/ppermute | solution.py:264
  101.5 52.3 %copy-start = (f32[1024]{0:T(1024)S(1)}, f32[1024]{0:T(1024)}, u32[]{:S(2)}) copy-start(f32[1024]{0:T(1024)} %param.3) | copy-start | bytes 12292
  146.2 7.6 %collective-permute-start.1 = (bf16[2304,128]{1,0:T(8,128)(2,1)S(1)}, bf16[2304,128]{1,0:T(8,128)(2,1)S(1)}, u32[]{:S(2)}, u32[]{:S(2)}) collective-permute-start(bf16[2304,128]{1,0:T(8,128)(2,1)S(1)} %bitcast.17), channel_id=1, source_target_pairs={{0,16},{16,0},{1,17},{17,1},{2,18},{18,2},{3,19},{19,3},{4,20},{20... | collective-permute-start | bytes 1769480 | tf_op jit(solution)/shard_map/ppermute | solution.py:274

commit v3 on v2

--- a/solution.py
+++ b/solution.py
@@ -14,14 +14,14 @@
 HALF = len(TILES) // 2
 ROWS = HALF * T
 HEAD = 8
-PLANE_SIZE = 16
-DEPTH = 16
-STRIP = ROWS // PLANE_SIZE
-PIECE = STRIP // DEPTH
-PAD = 16
+BLOCK_SIZE = 32
+BLOCKS = 8
+STRIP = ROWS // BLOCK_SIZE
+SLAB = STRIP + HEAD
 GROUP = 32
-MEM = ("z", "core")
+MEM = ("zo", "zi", "core")
 PLANE = ("y", "x")
+BLOCK = ("zi", "y", "x")
 
 
 def eye_mask():
@@ -89,75 +89,80 @@
     )(core, relaid)
 
 
-def pack_kernel(keep_ref, recv_ref, out_ref):
-    head = keep_ref[ROWS:, :] + recv_ref[ROWS:, :]
-    bound = jnp.maximum(head[1:2, :], 1e-30)
-    power = jnp.floor(15.0 - jnp.log2(bound))
-    scale = jnp.exp2(power)
-    share = head[0:1, :] * scale * 2.0**-20
+def scaling(bound):
+    power = jnp.floor(15.0 - jnp.log2(jnp.maximum(bound, 1e-30)))
+    return power, jnp.exp2(power)
+
+
+def tail_rows(power, scale, total):
+    share = total * scale * 2.0**-20
     high = share.astype(jnp.bfloat16).astype(jnp.float32)
     middle = (share - high).astype(jnp.bfloat16).astype(jnp.float32)
     low = share - high - middle
-    row = lax.broadcasted_iota(jnp.int32, (PAD, T), 0)
-    tail = jnp.zeros((PAD, T), jnp.float32)
+    row = lax.broadcasted_iota(jnp.int32, (HEAD, T), 0)
+    tail = jnp.zeros((HEAD, T), jnp.float32)
     for index, value in enumerate((power, high, middle, low)):
         tail = jnp.where(row == index, value, tail)
-    for p in range(PLANE_SIZE):
-        rows = slice(p * STRIP, (p + 1) * STRIP)
-        out_ref[p, :STRIP, :] = (keep_ref[rows, :] + recv_ref[rows, :]) * scale
-        out_ref[p, STRIP:, :] = tail
-
-
-def strip_kernel(parts_ref, out_ref, strip):
+    return tail
+
+
+def summed(parts_ref):
     acc = jnp.zeros((STRIP, T), jnp.float32)
     total = jnp.zeros((1, T), jnp.float32)
-    for p in range(PLANE_SIZE):
+    for p in range(parts_ref.shape[0]):
         tail = parts_ref[p, STRIP:, :]
         inverse = jnp.exp2(-tail[0:1, :])
         acc += parts_ref[p, :STRIP, :] * inverse
         total += (tail[1:2, :] + tail[2:3, :] + tail[3:4, :]) * inverse
-    strip[:STRIP, :] = acc
-    strip[STRIP:, :] = jnp.zeros((PAD, T), jnp.float32)
-    row = lax.broadcasted_iota(jnp.int32, (PAD, T), 0)
-    total = total * 2.0**20
-    for g in range(DEPTH):
-        piece = strip[g * PIECE:g * PIECE + PAD, :]
-        out_ref[g, :, :] = jnp.where(row == PIECE, total, piece)
-
-
-def entries_kernel(pieces_ref, out_ref):
-    whole = jnp.sum(pieces_ref[...], axis=0)
-    mean = whole[PIECE:PIECE + 1, :] / (M * (M - 1))
-    entries = jnp.exp(whole * (-1.0 / (0.08 * mean))).astype(jnp.bfloat16)
-    for g in range(DEPTH):
-        out_ref[g, :, :] = entries
-
-
-def spread_kernel(pieces_ref, out_ref, strip):
-    for g in range(DEPTH):
-        strip[g * PIECE:g * PIECE + PAD, :] = pieces_ref[g, :, :].astype(jnp.float32)
-    entries = strip[:STRIP, :].astype(jnp.bfloat16)
-    for p in range(PLANE_SIZE):
+    return acc, total * 2.0**20
+
+
+def pack_kernel(keep_ref, recv_ref, out_ref):
+    head = keep_ref[ROWS:, :] + recv_ref[ROWS:, :]
+    power, scale = scaling(head[1:2, :])
+    tail = tail_rows(power, scale, head[0:1, :])
+    for p in range(BLOCK_SIZE):
+        rows = slice(p * STRIP, (p + 1) * STRIP)
+        out_ref[p, :STRIP, :] = (keep_ref[rows, :] + recv_ref[rows, :]) * scale
+        out_ref[p, STRIP:, :] = tail
+
+
+def strip_kernel(parts_ref, out_ref):
+    acc, total = summed(parts_ref)
+    power, scale = scaling(jnp.maximum(jnp.max(acc, keepdims=True), total * 2.0**-20))
+    tail = tail_rows(power, scale, total)
+    acc = acc * scale
+    for g in range(BLOCKS):
+        out_ref[g, :STRIP, :] = acc
+        out_ref[g, STRIP:, :] = tail
+
+
+def entries_kernel(parts_ref, out_ref):
+    acc, total = summed(parts_ref)
+    mean = total / (M * (M - 1))
+    entries = jnp.exp(acc * (-1.0 / (0.08 * mean)))
+    entries = jnp.concatenate([entries, jnp.zeros((HEAD, T), jnp.float32)], axis=0)
+    entries = entries.astype(jnp.bfloat16)
+    for p in range(BLOCK_SIZE):
         out_ref[p, :, :] = entries
 
 
-def small_call(body, shape, dtype, name, scratch=()):
+def small_call(body, shape, dtype, name):
     return pl.pallas_call(
         body,
         out_shape=jax.ShapeDtypeStruct(shape, dtype),
-        scratch_shapes=scratch,
         compiler_params=pltpu.CompilerParams(vmem_limit_bytes=16 << 20),
         name=name,
     )
 
 
 def analysis_kernel(core_ref, own_ref, other_ref, logw_ref, relaid_ref, out_ref,
-                    packed, kern, weight, scale, coup, sems):
+                    packed, kern, weight, scale, coup):
     core = core_ref[0]
-    first = pltpu.make_async_copy(own_ref, packed.at[core], sems.at[0])
-    second = pltpu.make_async_copy(other_ref, packed.at[1 - core], sems.at[1])
-    first.start()
-    second.start()
+    for p in range(BLOCK_SIZE):
+        rows = slice(p * STRIP, (p + 1) * STRIP)
+        packed[core, rows, :] = own_ref[p].astype(jnp.float32)[:STRIP, :]
+        packed[1 - core, rows, :] = other_ref[p].astype(jnp.float32)[:STRIP, :]
     eye = eye_mask()
 
     def to_column(row):
@@ -169,15 +174,12 @@
     for i in range(NB):
         weight[i * T:(i + 1) * T, :] = to_column(weights[:, i * T:(i + 1) * T])
 
-    first.wait()
-    second.wait()
-
     def tile_of(i, j):
         half, slot = divmod(TILES.index((i, j)), HALF)
         return packed[half, slot * T:(slot + 1) * T, :]
 
     for i, j in TILES:
-        value = tile_of(i, j).astype(jnp.float32)
+        value = tile_of(i, j)
         kern[i * T:(i + 1) * T, j * T:(j + 1) * T] = value
         if i != j:
             kern[j * T:(j + 1) * T, i * T:(i + 1) * T] = value.T
@@ -229,31 +231,26 @@
 
 
 def analysis_members(core, own, other, log_weights, relaid):
+    vmem = pl.BlockSpec(memory_space=pltpu.VMEM)
     return pl.pallas_call(
         analysis_kernel,
         out_shape=jax.ShapeDtypeStruct(relaid.shape, jnp.bfloat16),
-        grid_spec=pltpu.PrefetchScalarGridSpec(
-            num_scalar_prefetch=1,
-            grid=(1,),
-            in_specs=[
-                pl.BlockSpec(memory_space=pl.ANY),
-                pl.BlockSpec(memory_space=pl.ANY),
-                pl.BlockSpec((1, M), lambda g, c: (0, 0)),
-                pl.BlockSpec(relaid.shape, lambda g, c: (0, 0)),
-            ],
-            out_specs=pl.BlockSpec(relaid.shape, lambda g, c: (0, 0)),
-            scratch_shapes=[
-                pltpu.VMEM((2, ROWS, T), jnp.bfloat16),
-                pltpu.VMEM((M, M), jnp.float32),
-                pltpu.VMEM((M, T), jnp.float32),
-                pltpu.VMEM((M, T), jnp.float32),
-                pltpu.VMEM((M, M), jnp.bfloat16),
-                pltpu.SemaphoreType.DMA((2,)),
-            ],
-        ),
+        in_specs=[pl.BlockSpec(memory_space=pltpu.SMEM), vmem, vmem, vmem, vmem],
+        out_specs=vmem,
+        scratch_shapes=[
+            pltpu.VMEM((2, ROWS, T), jnp.float32),
+            pltpu.VMEM((M, M), jnp.float32),
+            pltpu.VMEM((M, T), jnp.float32),
+            pltpu.VMEM((M, T), jnp.float32),
+            pltpu.VMEM((M, M), jnp.bfloat16),
+        ],
         compiler_params=pltpu.CompilerParams(vmem_limit_bytes=40 << 20),
         name="analysis",
     )(core, own, other, log_weights, relaid)
+
+
+def exchange(values, axes):
+    return lax.all_to_all(values, axes, 0, 0, tiled=True)
 
 
 def per_device(ensemble, log_weights):
@@ -262,22 +259,19 @@
     relaid = lax.all_to_all(ensemble, MEM, split_axis=1, concat_axis=0, tiled=True)
     keep, send = partial_distances(core, relaid)
     recv = lax.ppermute(send, "core", swap)
-    padded = pltpu.VMEM((STRIP + PAD, T), jnp.float32)
-    halves = small_call(pack_kernel, (PLANE_SIZE, STRIP + PAD, T), jnp.float32, "pack")(keep, recv)
-    parts = lax.all_to_all(halves.astype(jnp.float16), PLANE, 0, 0, tiled=True).astype(jnp.float32)
-    strips = small_call(strip_kernel, (DEPTH, PAD, T), jnp.float32, "strip", [padded])(parts)
-    pieces = lax.all_to_all(strips, "z", 0, 0, tiled=True)
-    entries = small_call(entries_kernel, (DEPTH, PAD, T), jnp.bfloat16, "entries")(pieces)
-    pieces = lax.all_to_all(entries, "z", 0, 0, tiled=True)
-    strips = small_call(spread_kernel, (PLANE_SIZE, STRIP, T), jnp.bfloat16, "spread", [padded])(pieces)
-    own = lax.all_to_all(strips, PLANE, 0, 0, tiled=True).reshape(ROWS, T)
+    slabs = small_call(pack_kernel, (BLOCK_SIZE, SLAB, T), jnp.float32, "pack")(keep, recv)
+    parts = exchange(slabs.astype(jnp.float16), BLOCK).astype(jnp.float32)
+    strips = small_call(strip_kernel, (BLOCKS, SLAB, T), jnp.float32, "strip")(parts)
+    parts = exchange(strips.astype(jnp.float16), "zo").astype(jnp.float32)
+    entries = small_call(entries_kernel, (BLOCK_SIZE, SLAB, T), jnp.bfloat16, "entries")(parts)
+    own = exchange(entries, BLOCK)
     other = lax.ppermute(own, "core", swap)
     mixed = analysis_members(core, own, other, log_weights.reshape(1, M), relaid)
     return lax.all_to_all(mixed, MEM, split_axis=0, concat_axis=1, tiled=True)
 
 
 def solution(mesh):
-    fine = Mesh(mesh.devices.reshape(16, 2, 4, 4), ("z", "core", "y", "x"))
+    fine = Mesh(mesh.devices.reshape(8, 2, 2, 4, 4), ("zo", "zi", "core", "y", "x"))
     return jax.shard_map(
         per_device,
         mesh=fine,

time: 224 us -> 213 us (0.951)
  blocking collectives: 122 us -> 110 us
    all_to_all x4 -> x3, blocking collectives: 63.5 us -> 49.3 us  [exchange(): return lax.all_to_all(values, axes, 0, 0, tiled=True)]
where the time goes in v3:
time: 213 us; the launch traced here: 212 us
  blocking collectives  110 us (52%)
  waiting for transfers between devices  59.9 us (28%)
  starting transfers between devices  26 us (12%)
  Pallas kernels  12.4 us (6%)
  local copies, waits for them, and re-layouts  3.41 us (2%)
    all_to_all x1, blocking collectives, per_device(): return lax.all_to_all(mixed, MEM, split_axis=0, concat_axis=1, tiled=True)  60.8 us
    all_to_all x1, waiting for transfers between devices, per_device(): lax.all_to_all(ensemble, MEM, split_axis=1, concat_axis=0, tiled=True)  55.7 us
    all_to_all x3, blocking collectives, exchange(): return lax.all_to_all(values, axes, 0, 0, tiled=True)  49.3 us
    all_to_all x1, starting transfers between devices, per_device(): lax.all_to_all(ensemble, MEM, split_axis=1, concat_axis=0, tiled=True)  16.7 us
    pallas_call x1, Pallas kernels, analysis_members(): pl.pallas_call(analysis_kernel, out_shape=jax.ShapeDtypeStruct(relaid.sha...  9.56 us
    ppermute x1, starting transfers between devices, per_device(): other = lax.ppermute(own, 'core', swap)  6.84 us
  transfers between devices with their start and end apart: 3, of which 3 were waited for; matrix products, arithmetic and copies ran while one was open for 0% of the time, Pallas kernels for 0%

profile of v3, /device:TPU:1, one launch (start us, length us, event | category | flops | bytes accessed | tf_op | source)
XLA Modules:
  0.0 212.1 jit_solution(5307179722465312977)
XLA Ops:
  0.0 2.3 %copy.8 = bf16[4,32,8,512]{3,2,0,1:T(8,128)(2,1)} copy(bf16[4,32,8,512]{3,2,1,0:T(8,128)(2,1)} %bitcast.18) | data formatting | bytes 2097152 | tf_op jit(solution)/shard_map/all_to_all | solution.py:259
  2.3 16.7 %all-to-all-start = ((bf16[32,32,512]{2,0,1:T(8,128)(2,1)}), bf16[32,32,512]{2,0,1:T(8,128)(2,1)S(1)}, u32[]{:S(2)}, u32[]{:S(2)}) async-start(bf16[32,32,512]{2,0,1:T(8,128)(2,1)} %bitcast.12), calls=%async_computation | async-start | bytes 2097152 | tf_op jit(solution)/shard_map/all_to_all | solution.py:259
  19.1 55.7 %all-to-all-done = bf16[32,32,512]{2,0,1:T(8,128)(2,1)S(1)} async-done(((bf16[32,32,512]{2,0,1:T(8,128)(2,1)}), bf16[32,32,512]{2,0,1:T(8,128)(2,1)S(1)}, u32[]{:S(2)}, u32[]{:S(2)}) %all-to-all-start) | async-done | bytes 1048608 | tf_op jit(solution)/shard_map/all_to_all | solution.py:259
  74.8 2.3 %distances.1 = (f32[2312,128]{1,0:T(8,128)S(1)}, f32[2312,128]{1,0:T(8,128)S(1)}) custom-call(s32[1]{0:T(128)} %bitcast.core_ref, bf16[1024,512]{1,0:T(8,128)(2,1)S(1)} %bitcast.13), custom_call_target="tpu_custom_call" | custom-call | tf_op jit(solution)/shard_map/distances/pallas_call | solution.py:74
  77.2 2.4 %collective-permute-start = (f32[2312,128]{1,0:T(8,128)S(1)}, f32[2312,128]{1,0:T(8,128)S(1)}, u32[]{:S(2)}, u32[]{:S(2)}) collective-permute-start(f32[2312,128]{1,0:T(8,128)S(1)} %get-tuple-element.8), channel_id=1, source_target_pairs={{0,16},{16,0},{1,17},{17,1},{2,18},{18,2},{3,19},{19,3},{4,20},{20... | collective-permute-start | bytes 3551240 | tf_op jit(solution)/shard_map/ppermute | solution.py:261
  79.6 2.5 %collective-permute-done.recv_ref = f32[2312,128]{1,0:T(8,128)S(1)} collective-permute-done((f32[2312,128]{1,0:T(8,128)S(1)}, f32[2312,128]{1,0:T(8,128)S(1)}, u32[]{:S(2)}, u32[]{:S(2)}) %collective-permute-start) | collective-permute-done | bytes 1183776 | tf_op jit(solution)/shard_map/ppermute | solution.py:261
  82.0 0.1 pack.1
  82.2 0.1 convert_element_type.12
  82.3 18.0 %all_to_all.53 = f16[32,80,128]{2,1,0:T(8,128)(2,1)S(1)} all-to-all(f16[32,80,128]{2,1,0:T(8,128)(2,1)S(1)} %convert_element_type.12), channel_id=1, replica_groups=mesh['zo'=8,'zi'=2,'core'=2,'y'=4,'x'=4] {'zi','y','x'}, dimensions={0} | all-to-all | bytes 1310720 | tf_op jit(solution)/shard_map/all_to_all | solution.py:253
  100.2 0.1 convert_element_type.13.parts_ref
  100.3 0.3 strip.1
  100.6 16.9 %all_to_all.54 = f16[8,80,128]{2,1,0:T(8,128)(2,1)S(1)} all-to-all(f16[8,80,128]{2,1,0:T(8,128)(2,1)S(1)} %convert_element_type.14), channel_id=1, replica_groups=mesh['zo'=8,'zi'=2,'core'=2,'y'=4,'x'=4] {'zo'}, dimensions={0} | all-to-all | bytes 327680 | tf_op jit(solution)/shard_map/all_to_all | solution.py:253
  117.5 0.0 copy-start
  117.5 0.1 entries.1
  117.6 14.5 %all_to_all.55.own_ref = bf16[32,80,128]{2,1,0:T(8,128)(2,1)S(1)} all-to-all(bf16[32,80,128]{2,1,0:T(8,128)(2,1)S(1)} %entries.1), channel_id=1, replica_groups=mesh['zo'=8,'zi'=2,'core'=2,'y'=4,'x'=4] {'zi','y','x'}, dimensions={0} | all-to-all | bytes 1310720 | tf_op jit(solution)/shard_map/all_to_all | solution.py:253
  132.1 6.8 %collective-permute-start.1 = (bf16[32,80,128]{2,1,0:T(8,128)(2,1)S(1)}, bf16[32,80,128]{2,1,0:T(8,128)(2,1)S(1)}, u32[]{:S(2)}, u32[]{:S(2)}) collective-permute-start(bf16[32,80,128]{2,1,0:T(8,128)(2,1)S(1)} %all_to_all.55.own_ref), channel_id=1, source_target_pairs={{0,16},{16,0},{1,17},{17,1},{2,18},{18,2},{3,19},{19,3},{4,20},{20... | collective-permute-start | bytes 1966088 | tf_op jit(solution)/shard_map/ppermute | solution.py:268
  139.0 1.7 collective-permute-done.1.other_ref
  140.7 0.0 copy-done
  140.7 9.6 %analysis.1 = bf16[1024,512]{1,0:T(8,128)(2,1)S(1)} custom-call(s32[1]{0:T(128)} %bitcast.core_ref, bf16[32,80,128]{2,1,0:T(8,128)(2,1)S(1)} %all_to_all.55.own_ref, bf16[32,80,128]{2,1,0:T(8,128)(2,1)S(1)} %collective-permute-done.1.other_ref, f32[1,1024]{1,0:T(1,128)S(1)} %bitcast.16, bf16[1024,512]{1,0:T(8,128)(2,1)S(1)} %bitcast.14), custom_call_target="tpu_custom_call" | custom-call | tf_op jit(solution)/shard_map/analysis/pallas_call | solution.py:235
  150.2 60.8 %all_to_all.56 = bf16[32,32,512]{2,1,0:T(8,128)(2,1)S(1)} all-to-all(bf16[32,32,512]{2,1,0:T(8,128)(2,1)S(1)} %bitcast.15), channel_id=1, replica_groups=mesh['zo'=8,'zi'=2,'core'=2,'y'=4,'x'=4] {'zo','zi','core'}, dimensions={0} | all-to-all | bytes 2097152 | tf_op jit(solution)/shard_map/all_to_all | solution.py:270
  211.0 1.1 copy.6
  (2 shorter events, 0.0 us)
Async XLA Ops:
  2.3 72.5 %all-to-all-start = ((bf16[32,32,512]{2,0,1:T(8,128)(2,1)}), bf16[32,32,512]{2,0,1:T(8,128)(2,1)S(1)}, u32[]{:S(2)}, u32[]{:S(2)}) async-start(bf16[32,32,512]{2,0,1:T(8,128)(2,1)} %bitcast.12), calls=%async_computation | async-start | bytes 2097152 | tf_op jit(solution)/shard_map/all_to_all | solution.py:259
  77.2 4.9 %collective-permute-start = (f32[2312,128]{1,0:T(8,128)S(1)}, f32[2312,128]{1,0:T(8,128)S(1)}, u32[]{:S(2)}, u32[]{:S(2)}) collective-permute-start(f32[2312,128]{1,0:T(8,128)S(1)} %get-tuple-element.8), channel_id=1, source_target_pairs={{0,16},{16,0},{1,17},{17,1},{2,18},{18,2},{3,19},{19,3},{4,20},{20... | collective-permute-start | bytes 3551240 | tf_op jit(solution)/shard_map/ppermute | solution.py:261
  117.5 23.1 %copy-start = (f32[1024]{0:T(1024)S(1)}, f32[1024]{0:T(1024)}, u32[]{:S(2)}) copy-start(f32[1024]{0:T(1024)} %param.3) | copy-start | bytes 12292
  132.1 8.5 %collective-permute-start.1 = (bf16[32,80,128]{2,1,0:T(8,128)(2,1)S(1)}, bf16[32,80,128]{2,1,0:T(8,128)(2,1)S(1)}, u32[]{:S(2)}, u32[]{:S(2)}) collective-permute-start(bf16[32,80,128]{2,1,0:T(8,128)(2,1)S(1)} %all_to_all.55.own_ref), channel_id=1, source_target_pairs={{0,16},{16,0},{1,17},{17,1},{2,18},{18,2},{3,19},{19,3},{4,20},{20... | collective-permute-start | bytes 1966088 | tf_op jit(solution)/shard_map/ppermute | solution.py:268

commit v4 on v3

--- a/solution.py
+++ b/solution.py
@@ -18,7 +18,8 @@
 BLOCKS = 8
 STRIP = ROWS // BLOCK_SIZE
 SLAB = STRIP + HEAD
-GROUP = 32
+SPLIT = 512
+GROUP = 16
 MEM = ("zo", "zi", "core")
 PLANE = ("y", "x")
 BLOCK = ("zi", "y", "x")
@@ -28,8 +29,49 @@
     return lax.broadcasted_iota(jnp.int32, (T, T), 0) == lax.broadcasted_iota(jnp.int32, (T, T), 1)
 
 
-def distance_kernel(core_ref, relaid_ref, keep_ref, send_ref, packed, sems):
-    core = core_ref[0]
+def split_kernel(ensemble_ref, out_ref):
+    count, _, cells = out_ref.shape
+    for d in range(count):
+        out_ref[d] = ensemble_ref[:, d * cells:(d + 1) * cells]
+
+
+def join_kernel(blocks_ref, out_ref, sems):
+    count, _, cells = blocks_ref.shape
+    copies = [
+        pltpu.make_async_copy(blocks_ref.at[d], out_ref.at[:, d * cells:(d + 1) * cells], sems.at[d])
+        for d in range(count)
+    ]
+    for copy in copies:
+        copy.start()
+    for copy in copies:
+        copy.wait()
+
+
+def split_cells(ensemble, shape):
+    return pl.pallas_call(
+        split_kernel,
+        out_shape=jax.ShapeDtypeStruct(shape, ensemble.dtype),
+        in_specs=[pl.BlockSpec(memory_space=pltpu.VMEM)],
+        out_specs=pl.BlockSpec(memory_space=pltpu.VMEM),
+        compiler_params=pltpu.CompilerParams(vmem_limit_bytes=8 << 20),
+        name="split",
+    )(ensemble)
+
+
+def join_cells(blocks, shape):
+    return pl.pallas_call(
+        join_kernel,
+        out_shape=jax.ShapeDtypeStruct(shape, blocks.dtype),
+        in_specs=[pl.BlockSpec(memory_space=pltpu.VMEM)],
+        out_specs=pl.BlockSpec(memory_space=pltpu.HBM),
+        scratch_shapes=[pltpu.SemaphoreType.DMA((blocks.shape[0],))],
+        compiler_params=pltpu.CompilerParams(vmem_limit_bytes=8 << 20),
+        name="join",
+    )(blocks)
+
+
+def distance_kernel(relaid_ref, keep_ref, send_ref, packed):
+    core = lax.axis_index("core")
     eye = eye_mask()
     norm_row = {}
     diagonal = jnp.zeros((8, T), jnp.float32)
@@ -61,32 +103,22 @@
     head = jnp.where(row == 0, total, jnp.where(row == 1, largest, 0.0))
     packed[0, ROWS:, :] = head
     packed[1, ROWS:, :] = head
-    keep = pltpu.make_async_copy(packed.at[core], keep_ref, sems.at[0])
-    send = pltpu.make_async_copy(packed.at[1 - core], send_ref, sems.at[1])
-    send.start()
-    keep.start()
-    send.wait()
-    keep.wait()
-
-
-def partial_distances(core, relaid):
+    keep_ref[...] = packed[core]
+    send_ref[...] = packed[1 - core]
+
+
+def partial_distances(relaid):
     shape = jax.ShapeDtypeStruct((ROWS + HEAD, T), jnp.float32)
+    vmem = pl.BlockSpec(memory_space=pltpu.VMEM)
     return pl.pallas_call(
         distance_kernel,
         out_shape=(shape, shape),
-        grid_spec=pltpu.PrefetchScalarGridSpec(
-            num_scalar_prefetch=1,
-            grid=(1,),
-            in_specs=[pl.BlockSpec(relaid.shape, lambda g, c: (0, 0))],
-            out_specs=(pl.BlockSpec(memory_space=pl.ANY), pl.BlockSpec(memory_space=pl.ANY)),
-            scratch_shapes=[
-                pltpu.VMEM((2, ROWS + HEAD, T), jnp.float32),
-                pltpu.SemaphoreType.DMA((2,)),
-            ],
-        ),
+        in_specs=[vmem],
+        out_specs=(vmem, vmem),
+        scratch_shapes=[pltpu.VMEM((2, ROWS + HEAD, T), jnp.float32)],
         compiler_params=pltpu.CompilerParams(vmem_limit_bytes=32 << 20),
         name="distances",
-    )(core, relaid)
+    )(relaid)
 
 
 def scaling(bound):
@@ -156,13 +188,30 @@
     )
 
 
-def analysis_kernel(core_ref, own_ref, other_ref, logw_ref, relaid_ref, out_ref,
-                    packed, kern, weight, scale, coup):
-    core = core_ref[0]
+def analysis_kernel(own_ref, other_ref, logw_ref, relaid_ref, out_ref,
+                    packed, kern_a, kern_at, kern_b, weight, scale, coup):
+    core = lax.axis_index("core")
     for p in range(BLOCK_SIZE):
         rows = slice(p * STRIP, (p + 1) * STRIP)
         packed[core, rows, :] = own_ref[p].astype(jnp.float32)[:STRIP, :]
         packed[1 - core, rows, :] = other_ref[p].astype(jnp.float32)[:STRIP, :]
+
+    def place(i, j, value):
+        cols = slice(j * T, (j + 1) * T)
+        if i * T < SPLIT:
+            kern_a[i * T:(i + 1) * T, cols] = value.astype(jnp.bfloat16)
+        else:
+            kern_b[i * T - SPLIT:(i + 1) * T - SPLIT, cols] = value
+        if j * T < SPLIT:
+            kern_at[i * T:(i + 1) * T, cols] = value.astype(jnp.bfloat16)
+
+    for tile, (i, j) in enumerate(TILES):
+        half, slot = divmod(tile, HALF)
+        value = packed[half, slot * T:(slot + 1) * T, :]
+        place(i, j, value)
+        if i != j:
+            place(j, i, value.T)
+
     eye = eye_mask()
 
     def to_column(row):
@@ -171,58 +220,58 @@
     logw = logw_ref[...]
     expw = jnp.exp(logw - jnp.max(logw, axis=1, keepdims=True))
     weights = expw / jnp.sum(expw, axis=1, keepdims=True)
-    for i in range(NB):
-        weight[i * T:(i + 1) * T, :] = to_column(weights[:, i * T:(i + 1) * T])
-
-    def tile_of(i, j):
-        half, slot = divmod(TILES.index((i, j)), HALF)
-        return packed[half, slot * T:(slot + 1) * T, :]
-
-    for i, j in TILES:
-        value = tile_of(i, j)
-        kern[i * T:(i + 1) * T, j * T:(j + 1) * T] = value
-        if i != j:
-            kern[j * T:(j + 1) * T, i * T:(i + 1) * T] = value.T
-
-    steps = M // (8 * GROUP)
-
-    def sweep(step, cols):
-        wide = [jnp.broadcast_to(c, (8, T)) for c in cols]
-
-        def block(b, sums):
-            base = pl.multiple_of(b * (8 * GROUP), 8 * GROUP)
+    for i in range(SPLIT // T, NB):
+        weight[i * T - SPLIT:(i + 1) * T - SPLIT, :] = to_column(weights[:, i * T:(i + 1) * T])
+
+    def product(vector, matrix):
+        first = vector.astype(jnp.bfloat16).astype(jnp.float32)
+        second = (vector - first).astype(jnp.bfloat16).astype(jnp.float32)
+        third = vector - first - second
+        row = lax.broadcasted_iota(jnp.int32, (16, vector.shape[1]), 0)
+        parts = jnp.where(row == 0, first, jnp.where(row == 1, second, jnp.where(row == 2, third, 0.0)))
+        sums = jnp.dot(parts.astype(jnp.bfloat16), matrix, preferred_element_type=jnp.float32)
+        return sums[0:1, :] + sums[1:2, :] + sums[2:3, :]
+
+    def sweep(step, scales):
+        scale_col = scales[1]
+        scale_a = weights[:, :SPLIT] / product(scale_col, kern_at[...])
+        from_a = product(scale_a, kern_a[...])
+        wide = [jnp.broadcast_to(scale_col[:, l * T:(l + 1) * T], (8, T)) for l in range(NB)]
+        sums = [jnp.zeros((8, T), jnp.float32) for _ in range(NB)]
+        for base in range(0, M - SPLIT, 8 * GROUP):
             row_scale = []
             for g in range(GROUP):
-                rows = pl.ds(base + 8 * g, 8)
-                acc = kern[rows, 0:T] * wide[0]
+                rows = slice(base + 8 * g, base + 8 * g + 8)
+                acc = kern_b[rows, 0:T] * wide[0]
                 for l in range(1, NB):
-                    acc += kern[rows, l * T:(l + 1) * T] * wide[l]
+                    acc += kern_b[rows, l * T:(l + 1) * T] * wide[l]
                 r = weight[rows, :] / jnp.sum(acc, axis=1, keepdims=True)
                 scale[rows, :] = r
                 row_scale.append(r)
-            sums = list(sums)
             for g in range(GROUP):
-                rows = pl.ds(base + 8 * g, 8)
+                rows = slice(base + 8 * g, base + 8 * g + 8)
                 for l in range(NB):
-                    sums[l] += kern[rows, l * T:(l + 1) * T] * row_scale[g]
-            return tuple(sums)
-
-        zeros = tuple(jnp.zeros((8, T), jnp.float32) for _ in range(NB))
-        sums = lax.fori_loop(0, steps, block, zeros)
-        return tuple((1.0 / M) / jnp.sum(s, axis=0, keepdims=True) for s in sums)
-
-    ones = tuple(jnp.ones((1, T), jnp.float32) for _ in range(NB))
-    cols = lax.fori_loop(0, ITERS, sweep, ones)
-
-    row_scale = [
-        M * jnp.sum(jnp.where(eye, scale[i * T:(i + 1) * T, :], 0.0), axis=0, keepdims=True)
-        for i in range(NB)
-    ]
+                    sums[l] += kern_b[rows, l * T:(l + 1) * T] * row_scale[g]
+        from_b = jnp.concatenate([jnp.sum(s, axis=0, keepdims=True) for s in sums], axis=1)
+        return scale_a, (1.0 / M) / (from_a + from_b)
+
+    start = (weights[:, :SPLIT], jnp.ones((1, M), jnp.float32))
+    scale_a, scale_col = lax.fori_loop(0, ITERS, sweep, start)
+
+    scale_row = [M * scale_a[:, i * T:(i + 1) * T] for i in range(SPLIT // T)]
+    for i in range(SPLIT // T, NB):
+        block = scale[i * T - SPLIT:(i + 1) * T - SPLIT, :]
+        scale_row.append(M * jnp.sum(jnp.where(eye, block, 0.0), axis=0, keepdims=True))
     for j in range(NB):
-        col_scale = to_column(cols[j])
+        rows = slice(j * T, (j + 1) * T)
+        column = to_column(scale_col[:, rows])
         for i in range(NB):
-            value = row_scale[i] * kern[j * T:(j + 1) * T, i * T:(i + 1) * T] * col_scale
-            coup[j * T:(j + 1) * T, i * T:(i + 1) * T] = value.astype(jnp.bfloat16)
+            cols = slice(i * T, (i + 1) * T)
+            if j * T < SPLIT:
+                value = kern_a[rows, cols].astype(jnp.float32)
+            else:
+                value = kern_b[j * T - SPLIT:(j + 1) * T - SPLIT, cols]
+            coup[rows, cols] = (scale_row[i] * value * column).astype(jnp.bfloat16)
     for j in range(0, NB, 2):
         mixed = jnp.dot(
             coup[j * T:(j + 2) * T, :], relaid_ref[...], preferred_element_type=jnp.float32
@@ -230,23 +279,25 @@
         out_ref[j * T:(j + 2) * T, :] = mixed.astype(jnp.bfloat16)
 
 
-def analysis_members(core, own, other, log_weights, relaid):
+def analysis_members(own, other, log_weights, relaid):
     vmem = pl.BlockSpec(memory_space=pltpu.VMEM)
     return pl.pallas_call(
         analysis_kernel,
         out_shape=jax.ShapeDtypeStruct(relaid.shape, jnp.bfloat16),
-        in_specs=[pl.BlockSpec(memory_space=pltpu.SMEM), vmem, vmem, vmem, vmem],
+        in_specs=[vmem, vmem, vmem, vmem],
         out_specs=vmem,
         scratch_shapes=[
             pltpu.VMEM((2, ROWS, T), jnp.float32),
-            pltpu.VMEM((M, M), jnp.float32),
-            pltpu.VMEM((M, T), jnp.float32),
-            pltpu.VMEM((M, T), jnp.float32),
+            pltpu.VMEM((SPLIT, M), jnp.bfloat16),
+            pltpu.VMEM((M, SPLIT), jnp.bfloat16),
+            pltpu.VMEM((M - SPLIT, M), jnp.float32),
+            pltpu.VMEM((M - SPLIT, T), jnp.float32),
+            pltpu.VMEM((M - SPLIT, T), jnp.float32),
             pltpu.VMEM((M, M), jnp.bfloat16),
         ],
         compiler_params=pltpu.CompilerParams(vmem_limit_bytes=40 << 20),
         name="analysis",
-    )(core, own, other, log_weights, relaid)
+    )(own, other, log_weights, relaid)
 
 
 def exchange(values, axes):
@@ -254,10 +305,13 @@
 
 
 def per_device(ensemble, log_weights):
-    core = lax.axis_index("core").reshape(1)
     swap = [(0, 1), (1, 0)]
-    relaid = lax.all_to_all(ensemble, MEM, split_axis=1, concat_axis=0, tiled=True)
-    keep, send = partial_distances(core, relaid)
+    rows, cells = ensemble.shape
+    count = M // rows
+    shape = (count, rows, cells // count)
+    blocks = split_cells(ensemble, shape)
+    relaid = exchange(blocks, MEM).reshape(M, cells // count)
+    keep, send = partial_distances(relaid)
     recv = lax.ppermute(send, "core", swap)
     slabs = small_call(pack_kernel, (BLOCK_SIZE, SLAB, T), jnp.float32, "pack")(keep, recv)
     parts = exchange(slabs.astype(jnp.float16), BLOCK).astype(jnp.float32)
@@ -266,8 +320,9 @@
     entries = small_call(entries_kernel, (BLOCK_SIZE, SLAB, T), jnp.bfloat16, "entries")(parts)
     own = exchange(entries, BLOCK)
     other = lax.ppermute(own, "core", swap)
-    mixed = analysis_members(core, own, other, log_weights.reshape(1, M), relaid)
-    return lax.all_to_all(mixed, MEM, split_axis=0, concat_axis=1, tiled=True)
+    mixed = analysis_members(own, other, log_weights.reshape(1, M), relaid)
+    blocks = exchange(mixed.reshape(shape), MEM)
+    return join_cells(blocks, ensemble.shape)
 
 
 def solution(mesh):

time: 213 us -> 210 us (0.986)
  blocking collectives: 110 us -> 182 us
  waiting for transfers between devices: 59.9 us -> 4.16 us
  starting transfers between devices: 26 us -> 9.23 us
  local copies, waits for them, and re-layouts: 3.41 us -> 1.23 us
    all_to_all x3 -> x5, blocking collectives: 49.3 us -> 182 us  [exchange(): return lax.all_to_all(values, axes, 0, 0, tiled=True)]
    all_to_all x1 -> x0, blocking collectives: 60.8 us -> none  [per_device(): return lax.all_to_all(mixed, MEM, split_axis=0, concat_axis=1, tiled=True)]
    all_to_all x1 -> x0, waiting for transfers between devices: 55.7 us -> none  [per_device(): lax.all_to_all(ensemble, MEM, split_axis=1, concat_axis=0, tiled=True)]
    all_to_all x1 -> x0, starting transfers between devices: 16.7 us -> none  [per_device(): lax.all_to_all(ensemble, MEM, split_axis=1, concat_axis=0, tiled=True)]
    all_to_all x2 -> x0, local copies, waits for them, and re-layouts: 3.4 us -> none  [the longest x1 2.33 us: per_device(): lax.all_to_all(ensemble, MEM, split_axis=1, concat_axis=0, tiled=True)]
  transfers between devices with their start and end apart: 3 -> 2, of which waited for: 3 -> 2; matrix products, arithmetic and copies ran while one was open for 0% -> 0% of each run, Pallas kernels for 0% -> 0%
where the time goes in v4:
time: 210 us
  blocking collectives  182 us (87%)
  Pallas kernels  12.5 us (6%)
  starting transfers between devices  9.23 us (4%)
  waiting for transfers between devices  4.16 us (2%)
    all_to_all x5, blocking collectives, exchange(): return lax.all_to_all(values, axes, 0, 0, tiled=True)  182 us
    pallas_call x1, Pallas kernels, analysis_members(): pl.pallas_call(analysis_kernel, out_shape=jax.ShapeDtypeStruct(relaid.sha...  8.51 us
    ppermute x1, starting transfers between devices, per_device(): other = lax.ppermute(own, 'core', swap)  6.81 us
  transfers between devices with their start and end apart: 2, of which 2 were waited for; matrix products, arithmetic and copies ran while one was open for 0% of the time, Pallas kernels for 0%

profile of v4, /device:TPU:1, one launch (start us, length us, event | category | flops | bytes accessed | tf_op | source)
XLA Modules:
  0.0 209.8 jit_solution(9565309603772513604)
XLA Ops:
  0.0 0.0 copy-start
  0.0 1.2 copy-done
  1.2 0.1 split.1
  1.3 72.3 %all_to_all.25 = bf16[32,32,512]{2,1,0:T(8,128)(2,1)S(1)} all-to-all(bf16[32,32,512]{2,1,0:T(8,128)(2,1)S(1)} %split.1), channel_id=1, replica_groups=mesh['zo'=8,'zi'=2,'core'=2,'y'=4,'x'=4] {'zo','zi','core'}, dimensions={0} | all-to-all | bytes 2097152 | tf_op jit(solution)/shard_map/all_to_all | solution.py:304
  73.6 2.2 %distances.1 = (f32[2312,128]{1,0:T(8,128)S(1)}, f32[2312,128]{1,0:T(8,128)S(1)}) custom-call(bf16[1024,512]{1,0:T(8,128)(2,1)S(1)} %bitcast.3), custom_call_target="tpu_custom_call" | custom-call | tf_op jit(solution)/shard_map/distances/pallas_call | solution.py:113
  75.8 2.4 %collective-permute-start = (f32[2312,128]{1,0:T(8,128)S(1)}, f32[2312,128]{1,0:T(8,128)S(1)}, u32[]{:S(2)}, u32[]{:S(2)}) collective-permute-start(f32[2312,128]{1,0:T(8,128)S(1)} %get-tuple-element.8), channel_id=1, source_target_pairs={{0,16},{16,0},{1,17},{17,1},{2,18},{18,2},{3,19},{19,3},{4,20},{20... | collective-permute-start | bytes 3551240 | tf_op jit(solution)/shard_map/ppermute | solution.py:315
  78.2 2.5 %collective-permute-done.recv_ref = f32[2312,128]{1,0:T(8,128)S(1)} collective-permute-done((f32[2312,128]{1,0:T(8,128)S(1)}, f32[2312,128]{1,0:T(8,128)S(1)}, u32[]{:S(2)}, u32[]{:S(2)}) %collective-permute-start) | collective-permute-done | bytes 1183776 | tf_op jit(solution)/shard_map/ppermute | solution.py:315
  80.7 0.1 pack.1
  80.8 0.1 convert_element_type.12
  80.9 18.0 %all_to_all.26 = f16[32,80,128]{2,1,0:T(8,128)(2,1)S(1)} all-to-all(f16[32,80,128]{2,1,0:T(8,128)(2,1)S(1)} %convert_element_type.12), channel_id=1, replica_groups=mesh['zo'=8,'zi'=2,'core'=2,'y'=4,'x'=4] {'zi','y','x'}, dimensions={0} | all-to-all | bytes 1310720 | tf_op jit(solution)/shard_map/all_to_all | solution.py:304
  98.9 0.1 convert_element_type.13.parts_ref
  99.0 0.3 strip.1
  99.3 16.8 %all_to_all.27 = f16[8,80,128]{2,1,0:T(8,128)(2,1)S(1)} all-to-all(f16[8,80,128]{2,1,0:T(8,128)(2,1)S(1)} %convert_element_type.14), channel_id=1, replica_groups=mesh['zo'=8,'zi'=2,'core'=2,'y'=4,'x'=4] {'zo'}, dimensions={0} | all-to-all | bytes 327680 | tf_op jit(solution)/shard_map/all_to_all | solution.py:304
  116.1 0.0 copy-start.1
  116.2 0.1 entries.1
  116.2 14.5 %all_to_all.28.own_ref = bf16[32,80,128]{2,1,0:T(8,128)(2,1)S(1)} all-to-all(bf16[32,80,128]{2,1,0:T(8,128)(2,1)S(1)} %entries.1), channel_id=1, replica_groups=mesh['zo'=8,'zi'=2,'core'=2,'y'=4,'x'=4] {'zi','y','x'}, dimensions={0} | all-to-all | bytes 1310720 | tf_op jit(solution)/shard_map/all_to_all | solution.py:304
  130.8 6.8 %collective-permute-start.1 = (bf16[32,80,128]{2,1,0:T(8,128)(2,1)S(1)}, bf16[32,80,128]{2,1,0:T(8,128)(2,1)S(1)}, u32[]{:S(2)}, u32[]{:S(2)}) collective-permute-start(bf16[32,80,128]{2,1,0:T(8,128)(2,1)S(1)} %all_to_all.28.own_ref), channel_id=1, source_target_pairs={{0,16},{16,0},{1,17},{17,1},{2,18},{18,2},{3,19},{19,3},{4,20},{20... | collective-permute-start | bytes 1966088 | tf_op jit(solution)/shard_map/ppermute | solution.py:322
  137.6 1.7 collective-permute-done.1.other_ref
  139.3 0.0 copy-done.1
  139.3 8.5 %analysis.1 = bf16[1024,512]{1,0:T(8,128)(2,1)S(1)} custom-call(bf16[32,80,128]{2,1,0:T(8,128)(2,1)S(1)} %all_to_all.28.own_ref, bf16[32,80,128]{2,1,0:T(8,128)(2,1)S(1)} %collective-permute-done.1.other_ref, f32[1,1024]{1,0:T(1,128)S(1)} %bitcast.6, bf16[1024,512]{1,0:T(8,128)(2,1)S(1)} %bitcast.4), custom_call_target="tpu_custom_call" | custom-call | tf_op jit(solution)/shard_map/analysis/pallas_call | solution.py:284
  147.8 60.8 %all_to_all.29.blocks_ref = bf16[32,32,512]{2,1,0:T(8,128)(2,1)S(1)} all-to-all(bf16[32,32,512]{2,1,0:T(8,128)(2,1)S(1)} %bitcast.5), channel_id=1, replica_groups=mesh['zo'=8,'zi'=2,'core'=2,'y'=4,'x'=4] {'zo','zi','core'}, dimensions={0} | all-to-all | bytes 2097152 | tf_op jit(solution)/shard_map/all_to_all | solution.py:304
  208.6 1.2 join.1
  (2 shorter events, 0.0 us)
Async XLA Ops:
  0.0 1.2 copy-start
  75.8 4.9 %collective-permute-start = (f32[2312,128]{1,0:T(8,128)S(1)}, f32[2312,128]{1,0:T(8,128)S(1)}, u32[]{:S(2)}, u32[]{:S(2)}) collective-permute-start(f32[2312,128]{1,0:T(8,128)S(1)} %get-tuple-element.8), channel_id=1, source_target_pairs={{0,16},{16,0},{1,17},{17,1},{2,18},{18,2},{3,19},{19,3},{4,20},{20... | collective-permute-start | bytes 3551240 | tf_op jit(solution)/shard_map/ppermute | solution.py:315
  116.1 23.2 %copy-start.1 = (f32[1024]{0:T(1024)S(1)}, f32[1024]{0:T(1024)}, u32[]{:S(2)}) copy-start(f32[1024]{0:T(1024)} %param.3) | copy-start | bytes 12292
  130.8 8.5 %collective-permute-start.1 = (bf16[32,80,128]{2,1,0:T(8,128)(2,1)S(1)}, bf16[32,80,128]{2,1,0:T(8,128)(2,1)S(1)}, u32[]{:S(2)}, u32[]{:S(2)}) collective-permute-start(bf16[32,80,128]{2,1,0:T(8,128)(2,1)S(1)} %all_to_all.28.own_ref), channel_id=1, source_target_pairs={{0,16},{16,0},{1,17},{17,1},{2,18},{18,2},{3,19},{19,3},{4,20},{20... | collective-permute-start | bytes 1966088 | tf_op jit(solution)/shard_map/ppermute | solution.py:322

commit v5 on v4

--- a/solution.py
+++ b/solution.py
@@ -7,6 +7,7 @@
 from jax.sharding import PartitionSpec as P
 
 M = 1024
+OWN = 32
 ITERS = 10
 T = 128
 NB = M // T
@@ -220,6 +221,9 @@
     logw = logw_ref[...]
     expw = jnp.exp(logw - jnp.max(logw, axis=1, keepdims=True))
     weights = expw / jnp.sum(expw, axis=1, keepdims=True)
+    weights = jnp.concatenate(
+        [weights[:, k * OWN:(k + 1) * OWN] for k in reversed(range(M // OWN))], axis=1
+    )
     for i in range(SPLIT // T, NB):
         weight[i * T - SPLIT:(i + 1) * T - SPLIT, :] = to_column(weights[:, i * T:(i + 1) * T])
 
@@ -304,24 +308,29 @@
     return lax.all_to_all(values, axes, 0, 0, tiled=True)
 
 
+def reversed_exchange(values, axes):
+    order = list(range(values.shape[0]))[::-1]
+    return lax.all_to_all(values, axes, 0, 0, tiled=True, axis_index_groups=[order])
+
+
 def per_device(ensemble, log_weights):
     swap = [(0, 1), (1, 0)]
     rows, cells = ensemble.shape
     count = M // rows
     shape = (count, rows, cells // count)
     blocks = split_cells(ensemble, shape)
-    relaid = exchange(blocks, MEM).reshape(M, cells // count)
+    relaid = reversed_exchange(blocks, MEM).reshape(M, cells // count)
     keep, send = partial_distances(relaid)
     recv = lax.ppermute(send, "core", swap)
     slabs = small_call(pack_kernel, (BLOCK_SIZE, SLAB, T), jnp.float32, "pack")(keep, recv)
     parts = exchange(slabs.astype(jnp.float16), BLOCK).astype(jnp.float32)
     strips = small_call(strip_kernel, (BLOCKS, SLAB, T), jnp.float32, "strip")(parts)
-    parts = exchange(strips.astype(jnp.float16), "zo").astype(jnp.float32)
+    parts = reversed_exchange(strips.astype(jnp.float16), "zo").astype(jnp.float32)
     entries = small_call(entries_kernel, (BLOCK_SIZE, SLAB, T), jnp.bfloat16, "entries")(parts)
     own = exchange(entries, BLOCK)
     other = lax.ppermute(own, "core", swap)
     mixed = analysis_members(own, other, log_weights.reshape(1, M), relaid)
-    blocks = exchange(mixed.reshape(shape), MEM)
+    blocks = reversed_exchange(mixed.reshape(shape), MEM)
     return join_cells(blocks, ensemble.shape)
 
 

time: 210 us -> 206 us (0.981)
  the two profiles are of different devices: /device:TPU:1 before, /device:TPU:33 now
where the time goes in v5:
time: 206 us
  blocking collectives  181 us (88%)
  Pallas kernels  12.6 us (6%)
  starting transfers between devices  6.93 us (3%)
  waiting for transfers between devices  4.16 us (2%)
    all_to_all x3, blocking collectives, reversed_exchange(): lax.all_to_all(values, axes, 0, 0, tiled=True, axis_index_groups=[order])  144 us
    all_to_all x2, blocking collectives, exchange(): return lax.all_to_all(values, axes, 0, 0, tiled=True)  36.3 us
    pallas_call x1, Pallas kernels, analysis_members(): pl.pallas_call(analysis_kernel, out_shape=jax.ShapeDtypeStruct(relaid.sha...  8.58 us
    ppermute x1, starting transfers between devices, per_device(): other = lax.ppermute(own, 'core', swap)  4.52 us
  transfers between devices with their start and end apart: 2, of which 2 were waited for; matrix products, arithmetic and copies ran while one was open for 0% of the time, Pallas kernels for 0%

profile of v5, /device:TPU:33, one launch (start us, length us, event | category | flops | bytes accessed | tf_op | source)
XLA Modules:
  0.0 205.8 jit_solution(8069151340169390038)
XLA Ops:
  0.0 0.0 copy-start
  0.0 1.2 copy-done
  1.2 0.1 split.1
  1.3 68.2 %all_to_all.25 = bf16[32,32,512]{2,1,0:T(8,128)(2,1)S(1)} all-to-all(bf16[32,32,512]{2,1,0:T(8,128)(2,1)S(1)} %split.1), channel_id=1, replica_groups={{496,480,464,448,432,416,400,384,368,352,336,320,304,288,272,256,240,22..., dimensions={0} | all-to-all | bytes 2097152 | tf_op jit(solution)/shard_map/all_to_all | solution.py:313
  69.5 2.2 %distances.1 = (f32[2312,128]{1,0:T(8,128)S(1)}, f32[2312,128]{1,0:T(8,128)S(1)}) custom-call(bf16[1024,512]{1,0:T(8,128)(2,1)S(1)} %bitcast.3), custom_call_target="tpu_custom_call" | custom-call | tf_op jit(solution)/shard_map/distances/pallas_call | solution.py:114
  71.7 2.4 %collective-permute-start = (f32[2312,128]{1,0:T(8,128)S(1)}, f32[2312,128]{1,0:T(8,128)S(1)}, u32[]{:S(2)}, u32[]{:S(2)}) collective-permute-start(f32[2312,128]{1,0:T(8,128)S(1)} %get-tuple-element.8), channel_id=1, source_target_pairs={{0,16},{16,0},{1,17},{17,1},{2,18},{18,2},{3,19},{19,3},{4,20},{20... | collective-permute-start | bytes 3551240 | tf_op jit(solution)/shard_map/ppermute | solution.py:324
  74.1 2.5 %collective-permute-done.recv_ref = f32[2312,128]{1,0:T(8,128)S(1)} collective-permute-done((f32[2312,128]{1,0:T(8,128)S(1)}, f32[2312,128]{1,0:T(8,128)S(1)}, u32[]{:S(2)}, u32[]{:S(2)}) %collective-permute-start) | collective-permute-done | bytes 1183776 | tf_op jit(solution)/shard_map/ppermute | solution.py:324
  76.6 0.1 pack.1
  76.7 0.1 convert_element_type.12
  76.8 19.0 %all_to_all.26 = f16[32,80,128]{2,1,0:T(8,128)(2,1)S(1)} all-to-all(f16[32,80,128]{2,1,0:T(8,128)(2,1)S(1)} %convert_element_type.12), channel_id=1, replica_groups=mesh['zo'=8,'zi'=2,'core'=2,'y'=4,'x'=4] {'zi','y','x'}, dimensions={0} | all-to-all | bytes 1310720 | tf_op jit(solution)/shard_map/all_to_all | solution.py:308
  95.8 0.1 convert_element_type.13.parts_ref
  95.9 0.3 strip.1
  96.2 17.1 %all_to_all.27 = f16[8,80,128]{2,1,0:T(8,128)(2,1)S(1)} all-to-all(f16[8,80,128]{2,1,0:T(8,128)(2,1)S(1)} %convert_element_type.14), channel_id=1, replica_groups={{448,384,320,256,192,128,64,0},{449,385,321,257,193,129,65,1},{450,386,..., dimensions={0} | all-to-all | bytes 327680 | tf_op jit(solution)/shard_map/all_to_all | solution.py:313
  113.4 0.0 copy-start.1
  113.4 0.1 entries.1
  113.5 17.3 %all_to_all.28.own_ref = bf16[32,80,128]{2,1,0:T(8,128)(2,1)S(1)} all-to-all(bf16[32,80,128]{2,1,0:T(8,128)(2,1)S(1)} %entries.1), channel_id=1, replica_groups=mesh['zo'=8,'zi'=2,'core'=2,'y'=4,'x'=4] {'zi','y','x'}, dimensions={0} | all-to-all | bytes 1310720 | tf_op jit(solution)/shard_map/all_to_all | solution.py:308
  130.8 4.5 %collective-permute-start.1 = (bf16[32,80,128]{2,1,0:T(8,128)(2,1)S(1)}, bf16[32,80,128]{2,1,0:T(8,128)(2,1)S(1)}, u32[]{:S(2)}, u32[]{:S(2)}) collective-permute-start(bf16[32,80,128]{2,1,0:T(8,128)(2,1)S(1)} %all_to_all.28.own_ref), channel_id=1, source_target_pairs={{0,16},{16,0},{1,17},{17,1},{2,18},{18,2},{3,19},{19,3},{4,20},{20... | collective-permute-start | bytes 1966088 | tf_op jit(solution)/shard_map/ppermute | solution.py:331
  135.3 1.7 collective-permute-done.1.other_ref
  137.0 0.0 copy-done.1
  137.0 8.6 %analysis.1 = bf16[1024,512]{1,0:T(8,128)(2,1)S(1)} custom-call(bf16[32,80,128]{2,1,0:T(8,128)(2,1)S(1)} %all_to_all.28.own_ref, bf16[32,80,128]{2,1,0:T(8,128)(2,1)S(1)} %collective-permute-done.1.other_ref, f32[1,1024]{1,0:T(1,128)S(1)} %bitcast.6, bf16[1024,512]{1,0:T(8,128)(2,1)S(1)} %bitcast.4), custom_call_target="tpu_custom_call" | custom-call | tf_op jit(solution)/shard_map/analysis/pallas_call | solution.py:288
  145.6 59.0 %all_to_all.29.blocks_ref = bf16[32,32,512]{2,1,0:T(8,128)(2,1)S(1)} all-to-all(bf16[32,32,512]{2,1,0:T(8,128)(2,1)S(1)} %bitcast.5), channel_id=1, replica_groups={{496,480,464,448,432,416,400,384,368,352,336,320,304,288,272,256,240,22..., dimensions={0} | all-to-all | bytes 2097152 | tf_op jit(solution)/shard_map/all_to_all | solution.py:313
  204.6 1.2 join.1
  (2 shorter events, 0.0 us)
Async XLA Ops:
  0.0 1.2 copy-start
  71.7 4.9 %collective-permute-start = (f32[2312,128]{1,0:T(8,128)S(1)}, f32[2312,128]{1,0:T(8,128)S(1)}, u32[]{:S(2)}, u32[]{:S(2)}) collective-permute-start(f32[2312,128]{1,0:T(8,128)S(1)} %get-tuple-element.8), channel_id=1, source_target_pairs={{0,16},{16,0},{1,17},{17,1},{2,18},{18,2},{3,19},{19,3},{4,20},{20... | collective-permute-start | bytes 3551240 | tf_op jit(solution)/shard_map/ppermute | solution.py:324
  113.4 23.7 %copy-start.1 = (f32[1024]{0:T(1024)S(1)}, f32[1024]{0:T(1024)}, u32[]{:S(2)}) copy-start(f32[1024]{0:T(1024)} %param.3) | copy-start | bytes 12292
  130.8 6.2 %collective-permute-start.1 = (bf16[32,80,128]{2,1,0:T(8,128)(2,1)S(1)}, bf16[32,80,128]{2,1,0:T(8,128)(2,1)S(1)}, u32[]{:S(2)}, u32[]{:S(2)}) collective-permute-start(bf16[32,80,128]{2,1,0:T(8,128)(2,1)S(1)} %all_to_all.28.own_ref), channel_id=1, source_target_pairs={{0,16},{16,0},{1,17},{17,1},{2,18},{18,2},{3,19},{19,3},{4,20},{20... | collective-permute-start | bytes 1966088 | tf_op jit(solution)/shard_map/ppermute | solution.py:331

commit v6 on v5

--- a/solution.py
+++ b/solution.py
@@ -78,34 +78,35 @@
     diagonal = jnp.zeros((8, T), jnp.float32)
     upper = jnp.zeros((8, T), jnp.float32)
     largest = jnp.zeros((8, T), jnp.float32)
-    for i in reversed(range(NB)):
-        rows = relaid_ref[i * T:(i + 1) * T, :]
+    for start in reversed(range(0, NB, 2)):
         strip = lax.dot_general(
-            rows, relaid_ref[i * T:, :], (((1,), (1,)), ((), ())), preferred_element_type=jnp.float32
+            relaid_ref[start * T:(start + 2) * T, :], relaid_ref[start * T:, :],
+            (((1,), (1,)), ((), ())), preferred_element_type=jnp.float32,
         )
-        own = jnp.where(eye, strip[:, :T], 0.0)
-        norm_row[i] = jnp.sum(own, axis=0, keepdims=True)
-        norm_col = jnp.sum(own, axis=1, keepdims=True)
-        for j in range(i, NB):
-            tile = TILES.index((i, j))
-            half, slot = divmod(tile, HALF)
-            gram = strip[:, (j - i) * T:(j - i + 1) * T]
-            value = norm_col + norm_row[j] - 2.0 * gram
-            packed[half, slot * T:(slot + 1) * T, :] = value
-            folded = value.reshape(T // 8, 8, T)
-            largest = jnp.maximum(largest, jnp.max(folded, axis=0))
-            if i == j:
-                diagonal += jnp.sum(folded, axis=0)
-            else:
-                upper += jnp.sum(folded, axis=0)
-    total = jnp.sum(diagonal + 2.0 * upper, keepdims=True)
-    largest = jnp.max(largest, keepdims=True)
+        for i in (start + 1, start):
+            rows = slice((i - start) * T, (i - start + 1) * T)
+            own = jnp.where(eye, strip[rows, rows], 0.0)
+            norm_row[i] = jnp.sum(own, axis=0, keepdims=True)
+            norm_col = jnp.sum(own, axis=1, keepdims=True)
+            for j in range(i, NB):
+                half, slot = divmod(TILES.index((i, j)), HALF)
+                gram = strip[rows, (j - start) * T:(j - start + 1) * T]
+                value = norm_col + norm_row[j] - 2.0 * gram
+                packed[half, slot * T:(slot + 1) * T, :] = value
+                folded = value.reshape(T // 8, 8, T)
+                largest = jnp.maximum(largest, jnp.max(folded, axis=0))
+                if i == j:
+                    diagonal += jnp.sum(folded, axis=0)
+                else:
+                    upper += jnp.sum(folded, axis=0)
+    total = jnp.broadcast_to(jnp.sum(diagonal + 2.0 * upper, keepdims=True), (1, T))
+    bound = jnp.broadcast_to(jnp.max(largest, keepdims=True), (1, T))
+    power, scale = scaling(bound)
     row = lax.broadcasted_iota(jnp.int32, (HEAD, T), 0)
-    head = jnp.where(row == 0, total, jnp.where(row == 1, largest, 0.0))
-    packed[0, ROWS:, :] = head
-    packed[1, ROWS:, :] = head
-    keep_ref[...] = packed[core]
-    send_ref[...] = packed[1 - core]
+    keep_ref[:ROWS, :] = packed[core]
+    keep_ref[ROWS:, :] = jnp.where(row == 0, total, jnp.where(row == 1, bound, 0.0))
+    send_ref[:ROWS, :] = packed[1 - core] * scale
+    send_ref[ROWS:, :] = tail_rows(power, scale, total)
 
 
 def partial_distances(relaid):
@@ -116,7 +117,7 @@
         out_shape=(shape, shape),
         in_specs=[vmem],
         out_specs=(vmem, vmem),
-        scratch_shapes=[pltpu.VMEM((2, ROWS + HEAD, T), jnp.float32)],
+        scratch_shapes=[pltpu.VMEM((2, ROWS, T), jnp.float32)],
         compiler_params=pltpu.CompilerParams(vmem_limit_bytes=32 << 20),
         name="distances",
     )(relaid)
@@ -139,6 +140,10 @@
     return tail
 
 
+def tail_total(tail, inverse):
+    return (tail[1:2, :] + tail[2:3, :] + tail[3:4, :]) * inverse * 2.0**20
+
+
 def summed(parts_ref):
     acc = jnp.zeros((STRIP, T), jnp.float32)
     total = jnp.zeros((1, T), jnp.float32)
@@ -146,17 +151,19 @@
         tail = parts_ref[p, STRIP:, :]
         inverse = jnp.exp2(-tail[0:1, :])
         acc += parts_ref[p, :STRIP, :] * inverse
-        total += (tail[1:2, :] + tail[2:3, :] + tail[3:4, :]) * inverse
-    return acc, total * 2.0**20
+        total += tail_total(tail, inverse)
+    return acc, total
 
 
 def pack_kernel(keep_ref, recv_ref, out_ref):
-    head = keep_ref[ROWS:, :] + recv_ref[ROWS:, :]
-    power, scale = scaling(head[1:2, :])
-    tail = tail_rows(power, scale, head[0:1, :])
+    other = recv_ref[ROWS:, :]
+    inverse = jnp.exp2(-other[0:1, :])
+    total = keep_ref[ROWS:ROWS + 1, :] + tail_total(other, inverse)
+    power, scale = scaling(keep_ref[ROWS + 1:ROWS + 2, :] + jnp.exp2(15.0 - other[0:1, :]))
+    tail = tail_rows(power, scale, total)
     for p in range(BLOCK_SIZE):
         rows = slice(p * STRIP, (p + 1) * STRIP)
-        out_ref[p, :STRIP, :] = (keep_ref[rows, :] + recv_ref[rows, :]) * scale
+        out_ref[p, :STRIP, :] = (keep_ref[rows, :] + recv_ref[rows, :] * inverse) * scale
         out_ref[p, STRIP:, :] = tail
 
 
@@ -321,7 +328,7 @@
     blocks = split_cells(ensemble, shape)
     relaid = reversed_exchange(blocks, MEM).reshape(M, cells // count)
     keep, send = partial_distances(relaid)
-    recv = lax.ppermute(send, "core", swap)
+    recv = lax.ppermute(send.astype(jnp.float16), "core", swap).astype(jnp.float32)
     slabs = small_call(pack_kernel, (BLOCK_SIZE, SLAB, T), jnp.float32, "pack")(keep, recv)
     parts = exchange(slabs.astype(jnp.float16), BLOCK).astype(jnp.float32)
     strips = small_call(strip_kernel, (BLOCKS, SLAB, T), jnp.float32, "strip")(parts)

time: 206 us -> 205 us (level)
  no operation moved by 1% of the time
where the time goes in v6:
time: 205 us
  blocking collectives  181 us (88%)
  Pallas kernels  12.1 us (6%)
  starting transfers between devices  6.92 us (3%)
  waiting for transfers between devices  3.31 us (2%)
    all_to_all x3, blocking collectives, reversed_exchange(): lax.all_to_all(values, axes, 0, 0, tiled=True, axis_index_groups=[order])  144 us
    all_to_all x2, blocking collectives, exchange(): return lax.all_to_all(values, axes, 0, 0, tiled=True)  36.3 us
    pallas_call x1, Pallas kernels, analysis_members(): pl.pallas_call(analysis_kernel, out_shape=jax.ShapeDtypeStruct(relaid.sha...  8.58 us
    ppermute x1, starting transfers between devices, per_device(): other = lax.ppermute(own, 'core', swap)  4.52 us
  transfers between devices with their start and end apart: 2, of which 2 were waited for; matrix products, arithmetic and copies ran while one was open for 0% of the time, Pallas kernels for 0%

profile of v6, /device:TPU:33, one launch (start us, length us, event | category | flops | bytes accessed | tf_op | source)
XLA Modules:
  0.0 204.6 jit_solution(13006032151421818001)
XLA Ops:
  0.0 0.0 copy-start
  0.0 1.2 copy-done
  1.2 0.1 split.1
  1.3 68.2 %all_to_all.25 = bf16[32,32,512]{2,1,0:T(8,128)(2,1)S(1)} all-to-all(bf16[32,32,512]{2,1,0:T(8,128)(2,1)S(1)} %split.1), channel_id=1, replica_groups={{496,480,464,448,432,416,400,384,368,352,336,320,304,288,272,256,240,22..., dimensions={0} | all-to-all | bytes 2097152 | tf_op jit(solution)/shard_map/all_to_all | solution.py:320
  69.5 1.6 distances.1
  71.2 0.1 convert_element_type.18
  71.3 2.4 %collective-permute-start = (f16[2312,128]{1,0:T(8,128)(2,1)S(1)}, f16[2312,128]{1,0:T(8,128)(2,1)S(1)}, u32[]{:S(2)}, u32[]{:S(2)}) collective-permute-start(f16[2312,128]{1,0:T(8,128)(2,1)S(1)} %convert_element_type.18), channel_id=1, source_target_pairs={{0,16},{16,0},{1,17},{17,1},{2,18},{18,2},{3,19},{19,3},{4,20},{20... | collective-permute-start | bytes 1775624 | tf_op jit(solution)/shard_map/ppermute | solution.py:331
  73.7 1.6 collective-permute-done
  75.3 0.1 convert_element_type.19.recv_ref
  75.4 0.2 pack.1
  75.5 0.1 convert_element_type.20
  75.6 19.0 %all_to_all.26 = f16[32,80,128]{2,1,0:T(8,128)(2,1)S(1)} all-to-all(f16[32,80,128]{2,1,0:T(8,128)(2,1)S(1)} %convert_element_type.20), channel_id=1, replica_groups=mesh['zo'=8,'zi'=2,'core'=2,'y'=4,'x'=4] {'zi','y','x'}, dimensions={0} | all-to-all | bytes 1310720 | tf_op jit(solution)/shard_map/all_to_all | solution.py:315
  94.7 0.1 convert_element_type.21.parts_ref
  94.8 0.3 strip.1
  95.1 17.1 %all_to_all.27 = f16[8,80,128]{2,1,0:T(8,128)(2,1)S(1)} all-to-all(f16[8,80,128]{2,1,0:T(8,128)(2,1)S(1)} %convert_element_type.22), channel_id=1, replica_groups={{448,384,320,256,192,128,64,0},{449,385,321,257,193,129,65,1},{450,386,..., dimensions={0} | all-to-all | bytes 327680 | tf_op jit(solution)/shard_map/all_to_all | solution.py:320
  112.2 0.0 copy-start.1
  112.2 0.1 entries.1
  112.3 17.3 %all_to_all.28.own_ref = bf16[32,80,128]{2,1,0:T(8,128)(2,1)S(1)} all-to-all(bf16[32,80,128]{2,1,0:T(8,128)(2,1)S(1)} %entries.1), channel_id=1, replica_groups=mesh['zo'=8,'zi'=2,'core'=2,'y'=4,'x'=4] {'zi','y','x'}, dimensions={0} | all-to-all | bytes 1310720 | tf_op jit(solution)/shard_map/all_to_all | solution.py:315
  129.6 4.5 %collective-permute-start.1 = (bf16[32,80,128]{2,1,0:T(8,128)(2,1)S(1)}, bf16[32,80,128]{2,1,0:T(8,128)(2,1)S(1)}, u32[]{:S(2)}, u32[]{:S(2)}) collective-permute-start(bf16[32,80,128]{2,1,0:T(8,128)(2,1)S(1)} %all_to_all.28.own_ref), channel_id=1, source_target_pairs={{0,16},{16,0},{1,17},{17,1},{2,18},{18,2},{3,19},{19,3},{4,20},{20... | collective-permute-start | bytes 1966088 | tf_op jit(solution)/shard_map/ppermute | solution.py:338
  134.2 1.7 collective-permute-done.1.other_ref
  135.9 0.0 copy-done.1
  135.9 8.6 %analysis.1 = bf16[1024,512]{1,0:T(8,128)(2,1)S(1)} custom-call(bf16[32,80,128]{2,1,0:T(8,128)(2,1)S(1)} %all_to_all.28.own_ref, bf16[32,80,128]{2,1,0:T(8,128)(2,1)S(1)} %collective-permute-done.1.other_ref, f32[1,1024]{1,0:T(1,128)S(1)} %bitcast.6, bf16[1024,512]{1,0:T(8,128)(2,1)S(1)} %bitcast.4), custom_call_target="tpu_custom_call" | custom-call | tf_op jit(solution)/shard_map/analysis/pallas_call | solution.py:295
  144.4 59.0 %all_to_all.29.blocks_ref = bf16[32,32,512]{2,1,0:T(8,128)(2,1)S(1)} all-to-all(bf16[32,32,512]{2,1,0:T(8,128)(2,1)S(1)} %bitcast.5), channel_id=1, replica_groups={{496,480,464,448,432,416,400,384,368,352,336,320,304,288,272,256,240,22..., dimensions={0} | all-to-all | bytes 2097152 | tf_op jit(solution)/shard_map/all_to_all | solution.py:320
  203.4 1.2 join.1
  (2 shorter events, 0.0 us)
Async XLA Ops:
  0.0 1.2 copy-start
  71.3 4.0 %collective-permute-start = (f16[2312,128]{1,0:T(8,128)(2,1)S(1)}, f16[2312,128]{1,0:T(8,128)(2,1)S(1)}, u32[]{:S(2)}, u32[]{:S(2)}) collective-permute-start(f16[2312,128]{1,0:T(8,128)(2,1)S(1)} %convert_element_type.18), channel_id=1, source_target_pairs={{0,16},{16,0},{1,17},{17,1},{2,18},{18,2},{3,19},{19,3},{4,20},{20... | collective-permute-start | bytes 1775624 | tf_op jit(solution)/shard_map/ppermute | solution.py:331
  112.2 23.7 %copy-start.1 = (f32[1024]{0:T(1024)S(1)}, f32[1024]{0:T(1024)}, u32[]{:S(2)}) copy-start(f32[1024]{0:T(1024)} %param.3) | copy-start | bytes 12292
  129.6 6.2 %collective-permute-start.1 = (bf16[32,80,128]{2,1,0:T(8,128)(2,1)S(1)}, bf16[32,80,128]{2,1,0:T(8,128)(2,1)S(1)}, u32[]{:S(2)}, u32[]{:S(2)}) collective-permute-start(bf16[32,80,128]{2,1,0:T(8,128)(2,1)S(1)} %all_to_all.28.own_ref), channel_id=1, source_target_pairs={{0,16},{16,0},{1,17},{17,1},{2,18},{18,2},{3,19},{19,3},{4,20},{20... | collective-permute-start | bytes 1966088 | tf_op jit(solution)/shard_map/ppermute | solution.py:338

commit v7 on v6

--- a/solution.py
+++ b/solution.py
@@ -8,6 +8,7 @@
 
 M = 1024
 OWN = 32
+ORDER = [2 * z + core for core in range(2) for z in reversed(range(16))]
 ITERS = 10
 T = 128
 NB = M // T
@@ -228,9 +229,7 @@
     logw = logw_ref[...]
     expw = jnp.exp(logw - jnp.max(logw, axis=1, keepdims=True))
     weights = expw / jnp.sum(expw, axis=1, keepdims=True)
-    weights = jnp.concatenate(
-        [weights[:, k * OWN:(k + 1) * OWN] for k in reversed(range(M // OWN))], axis=1
-    )
+    weights = jnp.concatenate([weights[:, k * OWN:(k + 1) * OWN] for k in ORDER], axis=1)
     for i in range(SPLIT // T, NB):
         weight[i * T - SPLIT:(i + 1) * T - SPLIT, :] = to_column(weights[:, i * T:(i + 1) * T])
 
@@ -315,8 +314,7 @@
     return lax.all_to_all(values, axes, 0, 0, tiled=True)
 
 
-def reversed_exchange(values, axes):
-    order = list(range(values.shape[0]))[::-1]
+def ordered_exchange(values, axes, order):
     return lax.all_to_all(values, axes, 0, 0, tiled=True, axis_index_groups=[order])
 
 
@@ -326,18 +324,18 @@
     count = M // rows
     shape = (count, rows, cells // count)
     blocks = split_cells(ensemble, shape)
-    relaid = reversed_exchange(blocks, MEM).reshape(M, cells // count)
+    relaid = ordered_exchange(blocks, MEM, ORDER).reshape(M, cells // count)
     keep, send = partial_distances(relaid)
     recv = lax.ppermute(send.astype(jnp.float16), "core", swap).astype(jnp.float32)
     slabs = small_call(pack_kernel, (BLOCK_SIZE, SLAB, T), jnp.float32, "pack")(keep, recv)
     parts = exchange(slabs.astype(jnp.float16), BLOCK).astype(jnp.float32)
     strips = small_call(strip_kernel, (BLOCKS, SLAB, T), jnp.float32, "strip")(parts)
-    parts = reversed_exchange(strips.astype(jnp.float16), "zo").astype(jnp.float32)
+    parts = ordered_exchange(strips.astype(jnp.float16), "zo", list(range(BLOCKS))[::-1]).astype(jnp.float32)
     entries = small_call(entries_kernel, (BLOCK_SIZE, SLAB, T), jnp.bfloat16, "entries")(parts)
     own = exchange(entries, BLOCK)
     other = lax.ppermute(own, "core", swap)
     mixed = analysis_members(own, other, log_weights.reshape(1, M), relaid)
-    blocks = reversed_exchange(mixed.reshape(shape), MEM)
+    blocks = ordered_exchange(mixed.reshape(shape), MEM, ORDER)
     return join_cells(blocks, ensemble.shape)
 
 

time: 205 us -> 203 us (level)
  the two profiles are of different devices: /device:TPU:33 before, /device:TPU:1 now
where the time goes in v7:
time: 203 us; the launch traced here: 202 us
  blocking collectives  178 us (88%)
  Pallas kernels  12.1 us (6%)
  starting transfers between devices  7.26 us (4%)
  waiting for transfers between devices  3.67 us (2%)
    all_to_all x3, blocking collectives, ordered_exchange(): lax.all_to_all(values, axes, 0, 0, tiled=True, axis_index_groups=[order])  139 us
    all_to_all x2, blocking collectives, exchange(): return lax.all_to_all(values, axes, 0, 0, tiled=True)  38.3 us
    pallas_call x1, Pallas kernels, analysis_members(): pl.pallas_call(analysis_kernel, out_shape=jax.ShapeDtypeStruct(relaid.sha...  8.6 us
    ppermute x1, starting transfers between devices, per_device(): other = lax.ppermute(own, 'core', swap)  5.34 us
  transfers between devices with their start and end apart: 2, of which 2 were waited for; matrix products, arithmetic and copies ran while one was open for 0% of the time, Pallas kernels for 0%

profile of v7, /device:TPU:1, one launch (start us, length us, event | category | flops | bytes accessed | tf_op | source)
XLA Modules:
  0.0 202.3 jit_solution(545481653454848714)
XLA Ops:
  0.0 0.0 copy-start
  0.0 1.2 copy-done
  1.2 0.1 split.1
  1.3 66.6 %all_to_all.25 = bf16[32,32,512]{2,1,0:T(8,128)(2,1)S(1)} all-to-all(bf16[32,32,512]{2,1,0:T(8,128)(2,1)S(1)} %split.1), channel_id=1, replica_groups={{480,448,416,384,352,320,288,256,224,192,160,128,96,64,32,0,496,464,432..., dimensions={0} | all-to-all | bytes 2097152 | tf_op jit(solution)/shard_map/all_to_all | solution.py:318
  67.9 1.6 distances.1
  69.6 0.1 convert_element_type.18
  69.7 1.9 collective-permute-start
  71.6 2.0 collective-permute-done
  73.6 0.1 convert_element_type.19.recv_ref
  73.7 0.2 pack.1
  73.8 0.1 convert_element_type.20
  73.9 18.4 %all_to_all.26 = f16[32,80,128]{2,1,0:T(8,128)(2,1)S(1)} all-to-all(f16[32,80,128]{2,1,0:T(8,128)(2,1)S(1)} %convert_element_type.20), channel_id=1, replica_groups=mesh['zo'=8,'zi'=2,'core'=2,'y'=4,'x'=4] {'zi','y','x'}, dimensions={0} | all-to-all | bytes 1310720 | tf_op jit(solution)/shard_map/all_to_all | solution.py:314
  92.4 0.1 convert_element_type.21.parts_ref
  92.5 0.3 strip.1
  92.8 17.4 %all_to_all.27 = f16[8,80,128]{2,1,0:T(8,128)(2,1)S(1)} all-to-all(f16[8,80,128]{2,1,0:T(8,128)(2,1)S(1)} %convert_element_type.22), channel_id=1, replica_groups={{448,384,320,256,192,128,64,0},{449,385,321,257,193,129,65,1},{450,386,..., dimensions={0} | all-to-all | bytes 327680 | tf_op jit(solution)/shard_map/all_to_all | solution.py:318
  110.3 0.0 copy-start.1
  110.3 0.1 entries.1
  110.4 19.9 %all_to_all.28.own_ref = bf16[32,80,128]{2,1,0:T(8,128)(2,1)S(1)} all-to-all(bf16[32,80,128]{2,1,0:T(8,128)(2,1)S(1)} %entries.1), channel_id=1, replica_groups=mesh['zo'=8,'zi'=2,'core'=2,'y'=4,'x'=4] {'zi','y','x'}, dimensions={0} | all-to-all | bytes 1310720 | tf_op jit(solution)/shard_map/all_to_all | solution.py:314
  130.3 5.3 %collective-permute-start.1 = (bf16[32,80,128]{2,1,0:T(8,128)(2,1)S(1)}, bf16[32,80,128]{2,1,0:T(8,128)(2,1)S(1)}, u32[]{:S(2)}, u32[]{:S(2)}) collective-permute-start(bf16[32,80,128]{2,1,0:T(8,128)(2,1)S(1)} %all_to_all.28.own_ref), channel_id=1, source_target_pairs={{0,16},{16,0},{1,17},{17,1},{2,18},{18,2},{3,19},{19,3},{4,20},{20... | collective-permute-start | bytes 1966088 | tf_op jit(solution)/shard_map/ppermute | solution.py:336
  135.6 1.7 collective-permute-done.1.other_ref
  137.3 0.0 copy-done.1
  137.3 8.6 %analysis.1 = bf16[1024,512]{1,0:T(8,128)(2,1)S(1)} custom-call(bf16[32,80,128]{2,1,0:T(8,128)(2,1)S(1)} %all_to_all.28.own_ref, bf16[32,80,128]{2,1,0:T(8,128)(2,1)S(1)} %collective-permute-done.1.other_ref, f32[1,1024]{1,0:T(1,128)S(1)} %bitcast.6, bf16[1024,512]{1,0:T(8,128)(2,1)S(1)} %bitcast.4), custom_call_target="tpu_custom_call" | custom-call | tf_op jit(solution)/shard_map/analysis/pallas_call | solution.py:294
  145.9 55.1 %all_to_all.29.blocks_ref = bf16[32,32,512]{2,1,0:T(8,128)(2,1)S(1)} all-to-all(bf16[32,32,512]{2,1,0:T(8,128)(2,1)S(1)} %bitcast.5), channel_id=1, replica_groups={{480,448,416,384,352,320,288,256,224,192,160,128,96,64,32,0,496,464,432..., dimensions={0} | all-to-all | bytes 2097152 | tf_op jit(solution)/shard_map/all_to_all | solution.py:318
  201.1 1.2 join.1
  (2 shorter events, 0.0 us)
Async XLA Ops:
  0.0 1.2 copy-start
  69.7 3.9 %collective-permute-start = (f16[2312,128]{1,0:T(8,128)(2,1)S(1)}, f16[2312,128]{1,0:T(8,128)(2,1)S(1)}, u32[]{:S(2)}, u32[]{:S(2)}) collective-permute-start(f16[2312,128]{1,0:T(8,128)(2,1)S(1)} %convert_element_type.18), channel_id=1, source_target_pairs={{0,16},{16,0},{1,17},{17,1},{2,18},{18,2},{3,19},{19,3},{4,20},{20... | collective-permute-start | bytes 1775624 | tf_op jit(solution)/shard_map/ppermute | solution.py:329
  110.3 27.0 %copy-start.1 = (f32[1024]{0:T(1024)S(1)}, f32[1024]{0:T(1024)}, u32[]{:S(2)}) copy-start(f32[1024]{0:T(1024)} %param.3) | copy-start | bytes 12292
  130.3 7.0 %collective-permute-start.1 = (bf16[32,80,128]{2,1,0:T(8,128)(2,1)S(1)}, bf16[32,80,128]{2,1,0:T(8,128)(2,1)S(1)}, u32[]{:S(2)}, u32[]{:S(2)}) collective-permute-start(bf16[32,80,128]{2,1,0:T(8,128)(2,1)S(1)} %all_to_all.28.own_ref), channel_id=1, source_target_pairs={{0,16},{16,0},{1,17},{17,1},{2,18},{18,2},{3,19},{19,3},{4,20},{20... | collective-permute-start | bytes 1966088 | tf_op jit(solution)/shard_map/ppermute | solution.py:336

commit v8 on v7

--- a/solution.py
+++ b/solution.py
@@ -8,7 +8,7 @@
 
 M = 1024
 OWN = 32
-ORDER = [2 * z + core for core in range(2) for z in reversed(range(16))]
+ORDER = [2 * z + core for core in (1, 0) for z in reversed(range(16))]
 ITERS = 10
 T = 128
 NB = M // T

time: 203 us -> 202 us (level)
  no operation moved by 1% of the time
where the time goes in v8:
time: 202 us; the launch traced here: 201 us
  blocking collectives  177 us (88%)
  Pallas kernels  12.1 us (6%)
  starting transfers between devices  7.26 us (4%)
  waiting for transfers between devices  3.67 us (2%)
    all_to_all x3, blocking collectives, ordered_exchange(): lax.all_to_all(values, axes, 0, 0, tiled=True, axis_index_groups=[order])  138 us
    all_to_all x2, blocking collectives, exchange(): return lax.all_to_all(values, axes, 0, 0, tiled=True)  38.5 us
    pallas_call x1, Pallas kernels, analysis_members(): pl.pallas_call(analysis_kernel, out_shape=jax.ShapeDtypeStruct(relaid.sha...  8.58 us
    ppermute x1, starting transfers between devices, per_device(): other = lax.ppermute(own, 'core', swap)  5.34 us
  transfers between devices with their start and end apart: 2, of which 2 were waited for; matrix products, arithmetic and copies ran while one was open for 0% of the time, Pallas kernels for 0%

profile of v8, /device:TPU:1, one launch (start us, length us, event | category | flops | bytes accessed | tf_op | source)
XLA Modules:
  0.0 201.3 jit_solution(3402253544621583049)
XLA Ops:
  0.0 0.0 copy-start
  0.0 1.2 copy-done
  1.2 0.1 split.1
  1.3 66.0 %all_to_all.25 = bf16[32,32,512]{2,1,0:T(8,128)(2,1)S(1)} all-to-all(bf16[32,32,512]{2,1,0:T(8,128)(2,1)S(1)} %split.1), channel_id=1, replica_groups={{496,464,432,400,368,336,304,272,240,208,176,144,112,80,48,16,480,448,4..., dimensions={0} | all-to-all | bytes 2097152 | tf_op jit(solution)/shard_map/all_to_all | solution.py:318
  67.3 1.6 distances.1
  69.0 0.1 convert_element_type.18
  69.0 1.9 collective-permute-start
  71.0 2.0 collective-permute-done
  72.9 0.1 convert_element_type.19.recv_ref
  73.0 0.2 pack.1
  73.2 0.1 convert_element_type.20
  73.3 18.6 %all_to_all.26 = f16[32,80,128]{2,1,0:T(8,128)(2,1)S(1)} all-to-all(f16[32,80,128]{2,1,0:T(8,128)(2,1)S(1)} %convert_element_type.20), channel_id=1, replica_groups=mesh['zo'=8,'zi'=2,'core'=2,'y'=4,'x'=4] {'zi','y','x'}, dimensions={0} | all-to-all | bytes 1310720 | tf_op jit(solution)/shard_map/all_to_all | solution.py:314
  91.9 0.1 convert_element_type.21.parts_ref
  92.0 0.3 strip.1
  92.3 17.6 %all_to_all.27 = f16[8,80,128]{2,1,0:T(8,128)(2,1)S(1)} all-to-all(f16[8,80,128]{2,1,0:T(8,128)(2,1)S(1)} %convert_element_type.22), channel_id=1, replica_groups={{448,384,320,256,192,128,64,0},{449,385,321,257,193,129,65,1},{450,386,..., dimensions={0} | all-to-all | bytes 327680 | tf_op jit(solution)/shard_map/all_to_all | solution.py:318
  109.9 0.0 copy-start.1
  110.0 0.1 entries.1
  110.1 19.9 %all_to_all.28.own_ref = bf16[32,80,128]{2,1,0:T(8,128)(2,1)S(1)} all-to-all(bf16[32,80,128]{2,1,0:T(8,128)(2,1)S(1)} %entries.1), channel_id=1, replica_groups=mesh['zo'=8,'zi'=2,'core'=2,'y'=4,'x'=4] {'zi','y','x'}, dimensions={0} | all-to-all | bytes 1310720 | tf_op jit(solution)/shard_map/all_to_all | solution.py:314
  129.9 5.3 %collective-permute-start.1 = (bf16[32,80,128]{2,1,0:T(8,128)(2,1)S(1)}, bf16[32,80,128]{2,1,0:T(8,128)(2,1)S(1)}, u32[]{:S(2)}, u32[]{:S(2)}) collective-permute-start(bf16[32,80,128]{2,1,0:T(8,128)(2,1)S(1)} %all_to_all.28.own_ref), channel_id=1, source_target_pairs={{0,16},{16,0},{1,17},{17,1},{2,18},{18,2},{3,19},{19,3},{4,20},{20... | collective-permute-start | bytes 1966088 | tf_op jit(solution)/shard_map/ppermute | solution.py:336
  135.3 1.7 collective-permute-done.1.other_ref
  137.0 0.0 copy-done.1
  137.0 8.6 %analysis.1 = bf16[1024,512]{1,0:T(8,128)(2,1)S(1)} custom-call(bf16[32,80,128]{2,1,0:T(8,128)(2,1)S(1)} %all_to_all.28.own_ref, bf16[32,80,128]{2,1,0:T(8,128)(2,1)S(1)} %collective-permute-done.1.other_ref, f32[1,1024]{1,0:T(1,128)S(1)} %bitcast.6, bf16[1024,512]{1,0:T(8,128)(2,1)S(1)} %bitcast.4), custom_call_target="tpu_custom_call" | custom-call | tf_op jit(solution)/shard_map/analysis/pallas_call | solution.py:294
  145.6 54.5 %all_to_all.29.blocks_ref = bf16[32,32,512]{2,1,0:T(8,128)(2,1)S(1)} all-to-all(bf16[32,32,512]{2,1,0:T(8,128)(2,1)S(1)} %bitcast.5), channel_id=1, replica_groups={{496,464,432,400,368,336,304,272,240,208,176,144,112,80,48,16,480,448,4..., dimensions={0} | all-to-all | bytes 2097152 | tf_op jit(solution)/shard_map/all_to_all | solution.py:318
  200.1 1.2 join.1
  (2 shorter events, 0.0 us)
Async XLA Ops:
  0.0 1.2 copy-start
  69.0 3.9 %collective-permute-start = (f16[2312,128]{1,0:T(8,128)(2,1)S(1)}, f16[2312,128]{1,0:T(8,128)(2,1)S(1)}, u32[]{:S(2)}, u32[]{:S(2)}) collective-permute-start(f16[2312,128]{1,0:T(8,128)(2,1)S(1)} %convert_element_type.18), channel_id=1, source_target_pairs={{0,16},{16,0},{1,17},{17,1},{2,18},{18,2},{3,19},{19,3},{4,20},{20... | collective-permute-start | bytes 1775624 | tf_op jit(solution)/shard_map/ppermute | solution.py:329
  109.9 27.0 %copy-start.1 = (f32[1024]{0:T(1024)S(1)}, f32[1024]{0:T(1024)}, u32[]{:S(2)}) copy-start(f32[1024]{0:T(1024)} %param.3) | copy-start | bytes 12292
  129.9 7.0 %collective-permute-start.1 = (bf16[32,80,128]{2,1,0:T(8,128)(2,1)S(1)}, bf16[32,80,128]{2,1,0:T(8,128)(2,1)S(1)}, u32[]{:S(2)}, u32[]{:S(2)}) collective-permute-start(bf16[32,80,128]{2,1,0:T(8,128)(2,1)S(1)} %all_to_all.28.own_ref), channel_id=1, source_target_pairs={{0,16},{16,0},{1,17},{17,1},{2,18},{18,2},{3,19},{19,3},{4,20},{20... | collective-permute-start | bytes 1966088 | tf_op jit(solution)/shard_map/ppermute | solution.py:336

commit v9 on v8

--- a/solution.py
+++ b/solution.py
@@ -12,7 +12,7 @@
 ITERS = 10
 T = 128
 NB = M // T
-TILES = [(i, j) for i in range(NB) for j in range(i, NB)]
+TILES = [(i, j) for i in range(NB) for j in range(i + 1, NB)] + [(i, i) for i in range(0, NB, 2)]
 HALF = len(TILES) // 2
 ROWS = HALF * T
 HEAD = 8
@@ -27,6 +27,10 @@
 BLOCK = ("zi", "y", "x")
 
 
+def above_mask():
+    return lax.broadcasted_iota(jnp.int32, (T, T), 0) < lax.broadcasted_iota(jnp.int32, (T, T), 1)
+
+
 def eye_mask():
     return lax.broadcasted_iota(jnp.int32, (T, T), 0) == lax.broadcasted_iota(jnp.int32, (T, T), 1)
 
@@ -76,31 +80,31 @@
     core = lax.axis_index("core")
     eye = eye_mask()
     norm_row = {}
-    diagonal = jnp.zeros((8, T), jnp.float32)
-    upper = jnp.zeros((8, T), jnp.float32)
+    sums = jnp.zeros((8, T), jnp.float32)
     largest = jnp.zeros((8, T), jnp.float32)
     for start in reversed(range(0, NB, 2)):
         strip = lax.dot_general(
             relaid_ref[start * T:(start + 2) * T, :], relaid_ref[start * T:, :],
             (((1,), (1,)), ((), ())), preferred_element_type=jnp.float32,
         )
+        values = {}
         for i in (start + 1, start):
             rows = slice((i - start) * T, (i - start + 1) * T)
             own = jnp.where(eye, strip[rows, rows], 0.0)
             norm_row[i] = jnp.sum(own, axis=0, keepdims=True)
             norm_col = jnp.sum(own, axis=1, keepdims=True)
             for j in range(i, NB):
-                half, slot = divmod(TILES.index((i, j)), HALF)
                 gram = strip[rows, (j - start) * T:(j - start + 1) * T]
-                value = norm_col + norm_row[j] - 2.0 * gram
-                packed[half, slot * T:(slot + 1) * T, :] = value
-                folded = value.reshape(T // 8, 8, T)
-                largest = jnp.maximum(largest, jnp.max(folded, axis=0))
-                if i == j:
-                    diagonal += jnp.sum(folded, axis=0)
-                else:
-                    upper += jnp.sum(folded, axis=0)
-    total = jnp.broadcast_to(jnp.sum(diagonal + 2.0 * upper, keepdims=True), (1, T))
+                values[i, j] = norm_col + norm_row[j] - 2.0 * gram
+        second = values.pop((start + 1, start + 1))
+        values[start, start] = jnp.where(above_mask(), values[start, start], second)
+        for tile, value in values.items():
+            half, slot = divmod(TILES.index(tile), HALF)
+            packed[half, slot * T:(slot + 1) * T, :] = value
+            folded = value.reshape(T // 8, 8, T)
+            largest = jnp.maximum(largest, jnp.max(folded, axis=0))
+            sums += jnp.sum(folded, axis=0)
+    total = jnp.broadcast_to(2.0 * jnp.sum(sums, keepdims=True), (1, T))
     bound = jnp.broadcast_to(jnp.max(largest, keepdims=True), (1, T))
     power, scale = scaling(bound)
     row = lax.broadcasted_iota(jnp.int32, (HEAD, T), 0)
@@ -181,9 +185,7 @@
 def entries_kernel(parts_ref, out_ref):
     acc, total = summed(parts_ref)
     mean = total / (M * (M - 1))
-    entries = jnp.exp(acc * (-1.0 / (0.08 * mean)))
-    entries = jnp.concatenate([entries, jnp.zeros((HEAD, T), jnp.float32)], axis=0)
-    entries = entries.astype(jnp.bfloat16)
+    entries = jnp.exp(acc * (-1.0 / (0.08 * mean))).astype(jnp.bfloat16)
     for p in range(BLOCK_SIZE):
         out_ref[p, :, :] = entries
 
@@ -202,8 +204,8 @@
     core = lax.axis_index("core")
     for p in range(BLOCK_SIZE):
         rows = slice(p * STRIP, (p + 1) * STRIP)
-        packed[core, rows, :] = own_ref[p].astype(jnp.float32)[:STRIP, :]
-        packed[1 - core, rows, :] = other_ref[p].astype(jnp.float32)[:STRIP, :]
+        packed[core, rows, :] = own_ref[p].astype(jnp.float32)
+        packed[1 - core, rows, :] = other_ref[p].astype(jnp.float32)
 
     def place(i, j, value):
         cols = slice(j * T, (j + 1) * T)
@@ -217,8 +219,12 @@
     for tile, (i, j) in enumerate(TILES):
         half, slot = divmod(tile, HALF)
         value = packed[half, slot * T:(slot + 1) * T, :]
-        place(i, j, value)
-        if i != j:
+        if i == j:
+            above = above_mask()
+            place(i, i, jnp.where(above, value, value.T))
+            place(i + 1, i + 1, jnp.where(above, value.T, value))
+        else:
+            place(i, j, value)
             place(j, i, value.T)
 
     eye = eye_mask()
@@ -331,7 +337,7 @@
     parts = exchange(slabs.astype(jnp.float16), BLOCK).astype(jnp.float32)
     strips = small_call(strip_kernel, (BLOCKS, SLAB, T), jnp.float32, "strip")(parts)
     parts = ordered_exchange(strips.astype(jnp.float16), "zo", list(range(BLOCKS))[::-1]).astype(jnp.float32)
-    entries = small_call(entries_kernel, (BLOCK_SIZE, SLAB, T), jnp.bfloat16, "entries")(parts)
+    entries = small_call(entries_kernel, (BLOCK_SIZE, STRIP, T), jnp.bfloat16, "entries")(parts)
     own = exchange(entries, BLOCK)
     other = lax.ppermute(own, "core", swap)
     mixed = analysis_members(own, other, log_weights.reshape(1, M), relaid)

time: 202 us -> 199 us (0.985)
  blocking collectives: 177 us -> 174 us
    all_to_all x2, blocking collectives: 38.5 us -> 35.3 us  [exchange(): return lax.all_to_all(values, axes, 0, 0, tiled=True)]
where the time goes in v9:
time: 199 us; the launch traced here: 198 us
  blocking collectives  174 us (87%)
  Pallas kernels  11.9 us (6%)
  starting transfers between devices  7.19 us (4%)
  waiting for transfers between devices  3.39 us (2%)
    all_to_all x3, blocking collectives, ordered_exchange(): lax.all_to_all(values, axes, 0, 0, tiled=True, axis_index_groups=[order])  139 us
    all_to_all x2, blocking collectives, exchange(): return lax.all_to_all(values, axes, 0, 0, tiled=True)  35.3 us
    pallas_call x1, Pallas kernels, analysis_members(): pl.pallas_call(analysis_kernel, out_shape=jax.ShapeDtypeStruct(relaid.sha...  8.46 us
    ppermute x1, starting transfers between devices, per_device(): other = lax.ppermute(own, 'core', swap)  5.27 us
  transfers between devices with their start and end apart: 2, of which 2 were waited for; matrix products, arithmetic and copies ran while one was open for 0% of the time, Pallas kernels for 0%

profile of v9, /device:TPU:1, one launch (start us, length us, event | category | flops | bytes accessed | tf_op | source)
XLA Modules:
  0.0 198.4 jit_solution(8829818703115924738)
XLA Ops:
  0.0 0.0 copy-start
  0.0 1.2 copy-done
  1.2 0.1 split.1
  1.3 66.0 %all_to_all.25 = bf16[32,32,512]{2,1,0:T(8,128)(2,1)S(1)} all-to-all(bf16[32,32,512]{2,1,0:T(8,128)(2,1)S(1)} %split.1), channel_id=1, replica_groups={{496,464,432,400,368,336,304,272,240,208,176,144,112,80,48,16,480,448,4..., dimensions={0} | all-to-all | bytes 2097152 | tf_op jit(solution)/shard_map/all_to_all | solution.py:324
  67.3 1.7 distances.1
  69.0 0.1 convert_element_type.18
  69.1 1.9 collective-permute-start
  71.0 1.9 collective-permute-done
  72.9 0.1 convert_element_type.19.recv_ref
  72.9 0.2 pack.1
  73.1 0.1 convert_element_type.20
  73.2 18.2 %all_to_all.26 = f16[32,72,128]{2,1,0:T(8,128)(2,1)S(1)} all-to-all(f16[32,72,128]{2,1,0:T(8,128)(2,1)S(1)} %convert_element_type.20), channel_id=1, replica_groups=mesh['zo'=8,'zi'=2,'core'=2,'y'=4,'x'=4] {'zi','y','x'}, dimensions={0} | all-to-all | bytes 1179648 | tf_op jit(solution)/shard_map/all_to_all | solution.py:320
  91.4 0.1 convert_element_type.21.parts_ref
  91.5 0.3 strip.1
  91.8 17.5 %all_to_all.27 = f16[8,72,128]{2,1,0:T(8,128)(2,1)S(1)} all-to-all(f16[8,72,128]{2,1,0:T(8,128)(2,1)S(1)} %convert_element_type.22), channel_id=1, replica_groups={{448,384,320,256,192,128,64,0},{449,385,321,257,193,129,65,1},{450,386,..., dimensions={0} | all-to-all | bytes 294912 | tf_op jit(solution)/shard_map/all_to_all | solution.py:324
  109.3 0.0 copy-start.1
  109.3 0.1 entries.1
  109.4 17.1 %all_to_all.28.own_ref = bf16[32,64,128]{2,1,0:T(8,128)(2,1)S(1)} all-to-all(bf16[32,64,128]{2,1,0:T(8,128)(2,1)S(1)} %entries.1), channel_id=1, replica_groups=mesh['zo'=8,'zi'=2,'core'=2,'y'=4,'x'=4] {'zi','y','x'}, dimensions={0} | all-to-all | bytes 1048576 | tf_op jit(solution)/shard_map/all_to_all | solution.py:320
  126.5 5.3 %collective-permute-start.1 = (bf16[32,64,128]{2,1,0:T(8,128)(2,1)S(1)}, bf16[32,64,128]{2,1,0:T(8,128)(2,1)S(1)}, u32[]{:S(2)}, u32[]{:S(2)}) collective-permute-start(bf16[32,64,128]{2,1,0:T(8,128)(2,1)S(1)} %all_to_all.28.own_ref), channel_id=1, source_target_pairs={{0,16},{16,0},{1,17},{17,1},{2,18},{18,2},{3,19},{19,3},{4,20},{20... | collective-permute-start | bytes 1572872 | tf_op jit(solution)/shard_map/ppermute | solution.py:342
  131.8 1.5 collective-permute-done.1.other_ref
  133.3 0.0 copy-done.1
  133.3 8.5 %analysis.1 = bf16[1024,512]{1,0:T(8,128)(2,1)S(1)} custom-call(bf16[32,64,128]{2,1,0:T(8,128)(2,1)S(1)} %all_to_all.28.own_ref, bf16[32,64,128]{2,1,0:T(8,128)(2,1)S(1)} %collective-permute-done.1.other_ref, f32[1,1024]{1,0:T(1,128)S(1)} %bitcast.6, bf16[1024,512]{1,0:T(8,128)(2,1)S(1)} %bitcast.4), custom_call_target="tpu_custom_call" | custom-call | tf_op jit(solution)/shard_map/analysis/pallas_call | solution.py:300
  141.8 55.4 %all_to_all.29.blocks_ref = bf16[32,32,512]{2,1,0:T(8,128)(2,1)S(1)} all-to-all(bf16[32,32,512]{2,1,0:T(8,128)(2,1)S(1)} %bitcast.5), channel_id=1, replica_groups={{496,464,432,400,368,336,304,272,240,208,176,144,112,80,48,16,480,448,4..., dimensions={0} | all-to-all | bytes 2097152 | tf_op jit(solution)/shard_map/all_to_all | solution.py:324
  197.1 1.2 join.1
  (2 shorter events, 0.0 us)
Async XLA Ops:
  0.0 1.2 copy-start
  69.1 3.8 %collective-permute-start = (f16[2056,128]{1,0:T(8,128)(2,1)S(1)}, f16[2056,128]{1,0:T(8,128)(2,1)S(1)}, u32[]{:S(2)}, u32[]{:S(2)}) collective-permute-start(f16[2056,128]{1,0:T(8,128)(2,1)S(1)} %convert_element_type.18), channel_id=1, source_target_pairs={{0,16},{16,0},{1,17},{17,1},{2,18},{18,2},{3,19},{19,3},{4,20},{20... | collective-permute-start | bytes 1579016 | tf_op jit(solution)/shard_map/ppermute | solution.py:335
  109.3 24.0 %copy-start.1 = (f32[1024]{0:T(1024)S(1)}, f32[1024]{0:T(1024)}, u32[]{:S(2)}) copy-start(f32[1024]{0:T(1024)} %param.3) | copy-start | bytes 12292
  126.5 6.8 %collective-permute-start.1 = (bf16[32,64,128]{2,1,0:T(8,128)(2,1)S(1)}, bf16[32,64,128]{2,1,0:T(8,128)(2,1)S(1)}, u32[]{:S(2)}, u32[]{:S(2)}) collective-permute-start(bf16[32,64,128]{2,1,0:T(8,128)(2,1)S(1)} %all_to_all.28.own_ref), channel_id=1, source_target_pairs={{0,16},{16,0},{1,17},{17,1},{2,18},{18,2},{3,19},{19,3},{4,20},{20... | collective-permute-start | bytes 1572872 | tf_op jit(solution)/shard_map/ppermute | solution.py:342

commit v10 on v9

--- a/solution.py
+++ b/solution.py
@@ -35,10 +35,16 @@
     return lax.broadcasted_iota(jnp.int32, (T, T), 0) == lax.broadcasted_iota(jnp.int32, (T, T), 1)
 
 
-def split_kernel(ensemble_ref, out_ref):
+def split_kernel(ensemble_ref, out_ref, sems):
     count, _, cells = out_ref.shape
-    for d in range(count):
-        out_ref[d] = ensemble_ref[:, d * cells:(d + 1) * cells]
+    copies = [
+        pltpu.make_async_copy(ensemble_ref.at[:, d * cells:(d + 1) * cells], out_ref.at[d], sems.at[d])
+        for d in range(count)
+    ]
+    for copy in copies:
+        copy.start()
+    for copy in copies:
+        copy.wait()
 
 
 def join_kernel(blocks_ref, out_ref, sems):
@@ -57,9 +63,10 @@
     return pl.pallas_call(
         split_kernel,
         out_shape=jax.ShapeDtypeStruct(shape, ensemble.dtype),
-        in_specs=[pl.BlockSpec(memory_space=pltpu.VMEM)],
+        in_specs=[pl.BlockSpec(memory_space=pltpu.HBM)],
         out_specs=pl.BlockSpec(memory_space=pltpu.VMEM),
-        compiler_params=pltpu.CompilerParams(vmem_limit_bytes=8 << 20),
+        scratch_shapes=[pltpu.SemaphoreType.DMA((shape[0],))],
+        compiler_params=pltpu.CompilerParams(vmem_limit_bytes=52 << 20),
         name="split",
     )(ensemble)
 

time: 199 us -> 199 us (level)
  no operation moved by 1% of the time
where the time goes in v10:
time: 199 us
  blocking collectives  174 us (87%)
  Pallas kernels  13.3 us (7%)
  starting transfers between devices  7.19 us (4%)
  waiting for transfers between devices  3.39 us (2%)
    all_to_all x3, blocking collectives, ordered_exchange(): lax.all_to_all(values, axes, 0, 0, tiled=True, axis_index_groups=[order])  139 us
    all_to_all x2, blocking collectives, exchange(): return lax.all_to_all(values, axes, 0, 0, tiled=True)  35.3 us
    pallas_call x1, Pallas kernels, analysis_members(): pl.pallas_call(analysis_kernel, out_shape=jax.ShapeDtypeStruct(relaid.sha...  8.46 us
    ppermute x1, starting transfers between devices, per_device(): other = lax.ppermute(own, 'core', swap)  5.27 us
  transfers between devices with their start and end apart: 2, of which 2 were waited for; matrix products, arithmetic and copies ran while one was open for 0% of the time, Pallas kernels for 0%

profile of v10, /device:TPU:1, one launch (start us, length us, event | category | flops | bytes accessed | tf_op | source)
XLA Modules:
  0.0 198.5 jit_solution(13667855229305765407)
XLA Ops:
  0.0 1.5 split.1
  1.5 66.0 %all_to_all.25 = bf16[32,32,512]{2,1,0:T(8,128)(2,1)S(1)} all-to-all(bf16[32,32,512]{2,1,0:T(8,128)(2,1)S(1)} %split.1), channel_id=1, replica_groups={{496,464,432,400,368,336,304,272,240,208,176,144,112,80,48,16,480,448,4..., dimensions={0} | all-to-all | bytes 2097152 | tf_op jit(solution)/shard_map/all_to_all | solution.py:331
  67.5 1.7 distances.1
  69.1 0.1 convert_element_type.18
  69.2 1.9 collective-permute-start
  71.2 1.9 collective-permute-done
  73.0 0.1 convert_element_type.19.recv_ref
  73.1 0.2 pack.1
  73.3 0.1 convert_element_type.20
  73.4 18.2 %all_to_all.26 = f16[32,72,128]{2,1,0:T(8,128)(2,1)S(1)} all-to-all(f16[32,72,128]{2,1,0:T(8,128)(2,1)S(1)} %convert_element_type.20), channel_id=1, replica_groups=mesh['zo'=8,'zi'=2,'core'=2,'y'=4,'x'=4] {'zi','y','x'}, dimensions={0} | all-to-all | bytes 1179648 | tf_op jit(solution)/shard_map/all_to_all | solution.py:327
  91.6 0.1 convert_element_type.21.parts_ref
  91.7 0.3 strip.1
  92.0 17.5 %all_to_all.27 = f16[8,72,128]{2,1,0:T(8,128)(2,1)S(1)} all-to-all(f16[8,72,128]{2,1,0:T(8,128)(2,1)S(1)} %convert_element_type.22), channel_id=1, replica_groups={{448,384,320,256,192,128,64,0},{449,385,321,257,193,129,65,1},{450,386,..., dimensions={0} | all-to-all | bytes 294912 | tf_op jit(solution)/shard_map/all_to_all | solution.py:331
  109.4 0.0 copy-start
  109.5 0.1 entries.1
  109.6 17.1 %all_to_all.28.own_ref = bf16[32,64,128]{2,1,0:T(8,128)(2,1)S(1)} all-to-all(bf16[32,64,128]{2,1,0:T(8,128)(2,1)S(1)} %entries.1), channel_id=1, replica_groups=mesh['zo'=8,'zi'=2,'core'=2,'y'=4,'x'=4] {'zi','y','x'}, dimensions={0} | all-to-all | bytes 1048576 | tf_op jit(solution)/shard_map/all_to_all | solution.py:327
  126.7 5.3 %collective-permute-start.1 = (bf16[32,64,128]{2,1,0:T(8,128)(2,1)S(1)}, bf16[32,64,128]{2,1,0:T(8,128)(2,1)S(1)}, u32[]{:S(2)}, u32[]{:S(2)}) collective-permute-start(bf16[32,64,128]{2,1,0:T(8,128)(2,1)S(1)} %all_to_all.28.own_ref), channel_id=1, source_target_pairs={{0,16},{16,0},{1,17},{17,1},{2,18},{18,2},{3,19},{19,3},{4,20},{20... | collective-permute-start | bytes 1572872 | tf_op jit(solution)/shard_map/ppermute | solution.py:349
  131.9 1.5 collective-permute-done.1.other_ref
  133.5 0.0 copy-done
  133.5 8.5 %analysis.1 = bf16[1024,512]{1,0:T(8,128)(2,1)S(1)} custom-call(bf16[32,64,128]{2,1,0:T(8,128)(2,1)S(1)} %all_to_all.28.own_ref, bf16[32,64,128]{2,1,0:T(8,128)(2,1)S(1)} %collective-permute-done.1.other_ref, f32[1,1024]{1,0:T(1,128)S(1)} %bitcast.6, bf16[1024,512]{1,0:T(8,128)(2,1)S(1)} %bitcast.4), custom_call_target="tpu_custom_call" | custom-call | tf_op jit(solution)/shard_map/analysis/pallas_call | solution.py:307
  141.9 55.4 %all_to_all.29.blocks_ref = bf16[32,32,512]{2,1,0:T(8,128)(2,1)S(1)} all-to-all(bf16[32,32,512]{2,1,0:T(8,128)(2,1)S(1)} %bitcast.5), channel_id=1, replica_groups={{496,464,432,400,368,336,304,272,240,208,176,144,112,80,48,16,480,448,4..., dimensions={0} | all-to-all | bytes 2097152 | tf_op jit(solution)/shard_map/all_to_all | solution.py:331
  197.3 1.2 join.1
  (2 shorter events, 0.0 us)
Async XLA Ops:
  69.2 3.8 %collective-permute-start = (f16[2056,128]{1,0:T(8,128)(2,1)S(1)}, f16[2056,128]{1,0:T(8,128)(2,1)S(1)}, u32[]{:S(2)}, u32[]{:S(2)}) collective-permute-start(f16[2056,128]{1,0:T(8,128)(2,1)S(1)} %convert_element_type.18), channel_id=1, source_target_pairs={{0,16},{16,0},{1,17},{17,1},{2,18},{18,2},{3,19},{19,3},{4,20},{20... | collective-permute-start | bytes 1579016 | tf_op jit(solution)/shard_map/ppermute | solution.py:342
  109.4 24.0 %copy-start = (f32[1024]{0:T(1024)S(1)}, f32[1024]{0:T(1024)}, u32[]{:S(2)}) copy-start(f32[1024]{0:T(1024)} %param.3) | copy-start | bytes 12292
  126.7 6.8 %collective-permute-start.1 = (bf16[32,64,128]{2,1,0:T(8,128)(2,1)S(1)}, bf16[32,64,128]{2,1,0:T(8,128)(2,1)S(1)}, u32[]{:S(2)}, u32[]{:S(2)}) collective-permute-start(bf16[32,64,128]{2,1,0:T(8,128)(2,1)S(1)} %all_to_all.28.own_ref), channel_id=1, source_target_pairs={{0,16},{16,0},{1,17},{17,1},{2,18},{18,2},{3,19},{19,3},{4,20},{20... | collective-permute-start | bytes 1572872 | tf_op jit(solution)/shard_map/ppermute | solution.py:349

commit v11 on v9

--- a/solution.py
+++ b/solution.py
@@ -41,18 +41,6 @@
         out_ref[d] = ensemble_ref[:, d * cells:(d + 1) * cells]
 
 
-def join_kernel(blocks_ref, out_ref, sems):
-    count, _, cells = blocks_ref.shape
-    copies = [
-        pltpu.make_async_copy(blocks_ref.at[d], out_ref.at[:, d * cells:(d + 1) * cells], sems.at[d])
-        for d in range(count)
-    ]
-    for copy in copies:
-        copy.start()
-    for copy in copies:
-        copy.wait()
-
-
 def split_cells(ensemble, shape):
     return pl.pallas_call(
         split_kernel,
@@ -62,18 +50,6 @@
         compiler_params=pltpu.CompilerParams(vmem_limit_bytes=8 << 20),
         name="split",
     )(ensemble)
-
-
-def join_cells(blocks, shape):
-    return pl.pallas_call(
-        join_kernel,
-        out_shape=jax.ShapeDtypeStruct(shape, blocks.dtype),
-        in_specs=[pl.BlockSpec(memory_space=pltpu.VMEM)],
-        out_specs=pl.BlockSpec(memory_space=pltpu.HBM),
-        scratch_shapes=[pltpu.SemaphoreType.DMA((blocks.shape[0],))],
-        compiler_params=pltpu.CompilerParams(vmem_limit_bytes=8 << 20),
-        name="join",
-    )(blocks)
 
 
 def distance_kernel(relaid_ref, keep_ref, send_ref, packed):
@@ -336,13 +312,13 @@
     slabs = small_call(pack_kernel, (BLOCK_SIZE, SLAB, T), jnp.float32, "pack")(keep, recv)
     parts = exchange(slabs.astype(jnp.float16), BLOCK).astype(jnp.float32)
     strips = small_call(strip_kernel, (BLOCKS, SLAB, T), jnp.float32, "strip")(parts)
-    parts = ordered_exchange(strips.astype(jnp.float16), "zo", list(range(BLOCKS))[::-1]).astype(jnp.float32)
+    parts = ordered_exchange(strips.astype(jnp.float16), "zo", [7, 1, 2, 6, 5, 0, 3, 4]).astype(jnp.float32)
     entries = small_call(entries_kernel, (BLOCK_SIZE, STRIP, T), jnp.bfloat16, "entries")(parts)
     own = exchange(entries, BLOCK)
     other = lax.ppermute(own, "core", swap)
     mixed = analysis_members(own, other, log_weights.reshape(1, M), relaid)
     blocks = ordered_exchange(mixed.reshape(shape), MEM, ORDER)
-    return join_cells(blocks, ensemble.shape)
+    return blocks.transpose(1, 0, 2).reshape(ensemble.shape)
 
 
 def solution(mesh):

time: 199 us -> 199 us (level)
  no operation moved by 1% of the time
where the time goes in v11:
time: 199 us
  blocking collectives  174 us (87%)
  Pallas kernels  10.7 us (5%)
  starting transfers between devices  7.75 us (4%)
  waiting for transfers between devices  3.39 us (2%)
  local copies, waits for them, and re-layouts  2.3 us (1%)
    all_to_all x3, blocking collectives, ordered_exchange(): lax.all_to_all(values, axes, 0, 0, tiled=True, axis_index_groups=[order])  139 us
    all_to_all x2, blocking collectives, exchange(): return lax.all_to_all(values, axes, 0, 0, tiled=True)  35 us
    pallas_call x1, Pallas kernels, analysis_members(): pl.pallas_call(analysis_kernel, out_shape=jax.ShapeDtypeStruct(relaid.sha...  8.47 us
    ppermute x1, starting transfers between devices, per_device(): other = lax.ppermute(own, 'core', swap)  5.83 us
  transfers between devices with their start and end apart: 2, of which 2 were waited for; matrix products, arithmetic and copies ran while one was open for 0% of the time, Pallas kernels for 0%

profile of v11, /device:TPU:1, one launch (start us, length us, event | category | flops | bytes accessed | tf_op | source)
XLA Modules:
  0.0 198.9 jit_solution(3367522917365962881)
XLA Ops:
  0.0 0.0 copy-start
  0.0 1.2 copy-done
  1.2 0.1 split.1
  1.3 66.0 %all_to_all.25 = bf16[32,32,512]{2,1,0:T(8,128)(2,1)S(1)} all-to-all(bf16[32,32,512]{2,1,0:T(8,128)(2,1)S(1)} %split.1), channel_id=1, replica_groups={{496,464,432,400,368,336,304,272,240,208,176,144,112,80,48,16,480,448,4..., dimensions={0} | all-to-all | bytes 2097152 | tf_op jit(solution)/shard_map/all_to_all | solution.py:300
  67.3 1.7 distances.1
  69.0 0.1 convert_element_type.18
  69.1 1.9 collective-permute-start
  71.0 1.9 collective-permute-done
  72.9 0.1 convert_element_type.19.recv_ref
  72.9 0.2 pack.1
  73.1 0.1 convert_element_type.20
  73.2 18.2 %all_to_all.26 = f16[32,72,128]{2,1,0:T(8,128)(2,1)S(1)} all-to-all(f16[32,72,128]{2,1,0:T(8,128)(2,1)S(1)} %convert_element_type.20), channel_id=1, replica_groups=mesh['zo'=8,'zi'=2,'core'=2,'y'=4,'x'=4] {'zi','y','x'}, dimensions={0} | all-to-all | bytes 1179648 | tf_op jit(solution)/shard_map/all_to_all | solution.py:296
  91.4 0.1 convert_element_type.21.parts_ref
  91.5 0.3 strip.1
  91.8 16.9 %all_to_all.27 = f16[8,72,128]{2,1,0:T(8,128)(2,1)S(1)} all-to-all(f16[8,72,128]{2,1,0:T(8,128)(2,1)S(1)} %convert_element_type.22), channel_id=1, replica_groups={{448,64,128,384,320,0,192,256},{449,65,129,385,321,1,193,257},{450,66,1..., dimensions={0} | all-to-all | bytes 294912 | tf_op jit(solution)/shard_map/all_to_all | solution.py:300
  108.7 0.0 copy-start.1
  108.8 0.1 entries.1
  108.8 16.8 %all_to_all.28.own_ref = bf16[32,64,128]{2,1,0:T(8,128)(2,1)S(1)} all-to-all(bf16[32,64,128]{2,1,0:T(8,128)(2,1)S(1)} %entries.1), channel_id=1, replica_groups=mesh['zo'=8,'zi'=2,'core'=2,'y'=4,'x'=4] {'zi','y','x'}, dimensions={0} | all-to-all | bytes 1048576 | tf_op jit(solution)/shard_map/all_to_all | solution.py:296
  125.6 5.8 %collective-permute-start.1 = (bf16[32,64,128]{2,1,0:T(8,128)(2,1)S(1)}, bf16[32,64,128]{2,1,0:T(8,128)(2,1)S(1)}, u32[]{:S(2)}, u32[]{:S(2)}) collective-permute-start(bf16[32,64,128]{2,1,0:T(8,128)(2,1)S(1)} %all_to_all.28.own_ref), channel_id=1, source_target_pairs={{0,16},{16,0},{1,17},{17,1},{2,18},{18,2},{3,19},{19,3},{4,20},{20... | collective-permute-start | bytes 1572872 | tf_op jit(solution)/shard_map/ppermute | solution.py:318
  131.5 1.5 collective-permute-done.1.other_ref
  133.0 0.0 copy-done.1
  133.0 8.5 %analysis.1 = bf16[1024,512]{1,0:T(8,128)(2,1)S(1)} custom-call(bf16[32,64,128]{2,1,0:T(8,128)(2,1)S(1)} %all_to_all.28.own_ref, bf16[32,64,128]{2,1,0:T(8,128)(2,1)S(1)} %collective-permute-done.1.other_ref, f32[1,1024]{1,0:T(1,128)S(1)} %bitcast.9, bf16[1024,512]{1,0:T(8,128)(2,1)S(1)} %bitcast.7), custom_call_target="tpu_custom_call" | custom-call | tf_op jit(solution)/shard_map/analysis/pallas_call | solution.py:276
  141.4 56.4 %all_to_all.29 = bf16[32,32,512]{2,1,0:T(8,128)(2,1)S(1)} all-to-all(bf16[32,32,512]{2,1,0:T(8,128)(2,1)S(1)} %bitcast.8), channel_id=1, replica_groups={{496,464,432,400,368,336,304,272,240,208,176,144,112,80,48,16,480,448,4..., dimensions={0} | all-to-all | bytes 2097152 | tf_op jit(solution)/shard_map/all_to_all | solution.py:300
  197.9 1.1 copy.4
  (2 shorter events, 0.0 us)
Async XLA Ops:
  0.0 1.2 copy-start
  69.1 3.8 %collective-permute-start = (f16[2056,128]{1,0:T(8,128)(2,1)S(1)}, f16[2056,128]{1,0:T(8,128)(2,1)S(1)}, u32[]{:S(2)}, u32[]{:S(2)}) collective-permute-start(f16[2056,128]{1,0:T(8,128)(2,1)S(1)} %convert_element_type.18), channel_id=1, source_target_pairs={{0,16},{16,0},{1,17},{17,1},{2,18},{18,2},{3,19},{19,3},{4,20},{20... | collective-permute-start | bytes 1579016 | tf_op jit(solution)/shard_map/ppermute | solution.py:311
  108.7 24.2 %copy-start.1 = (f32[1024]{0:T(1024)S(1)}, f32[1024]{0:T(1024)}, u32[]{:S(2)}) copy-start(f32[1024]{0:T(1024)} %param.3) | copy-start | bytes 12292
  125.6 7.4 %collective-permute-start.1 = (bf16[32,64,128]{2,1,0:T(8,128)(2,1)S(1)}, bf16[32,64,128]{2,1,0:T(8,128)(2,1)S(1)}, u32[]{:S(2)}, u32[]{:S(2)}) collective-permute-start(bf16[32,64,128]{2,1,0:T(8,128)(2,1)S(1)} %all_to_all.28.own_ref), channel_id=1, source_target_pairs={{0,16},{16,0},{1,17},{17,1},{2,18},{18,2},{3,19},{19,3},{4,20},{20... | collective-permute-start | bytes 1572872 | tf_op jit(solution)/shard_map/ppermute | solution.py:318
